TPU v7x, 32 devices: a whole 2x2x4 slice. The times are simulated.
32 devices in a mesh: rows: 8 (over y, x, core), cols: 4 (over z).
Axes of the slice: x: 2, y: 2, z: 4, core: 2. Of those that a mesh axis runs over, the one named last changes fastest.
Arguments:
- grad: bfloat16 [28672, 8192], P(('rows', 'cols')), may hold values from -8 to 8
- momentum: float32 [28672, 8192], P('rows', 'cols'), may hold values from -8 to 8
- right_basis: bfloat16 [8192, 512], P('cols'), may hold values from -0.0625 to 0.0625
Outputs:
- momentum_new: float32 [28672, 8192], P('rows', 'cols')
- left_factor: float32 [28672, 512], P('rows')
- right_new: bfloat16 [8192, 512], P('cols')
All inputs are finite; a program needn't handle non-finite values.
Results may differ from a plain program's by a relative error of at most 0.01225.
Values may be sent and summed in bfloat16 or wider, within the bound.
A program may use at most 192 MiB of HBM per device.

v0:
```python
import jax
import jax.numpy as jnp
from jax import lax
from jax.sharding import PartitionSpec as P

epsilon = 1e-06
feedback_weight = 0.05


def partner_2(x, axis, stride):
    return lax.ppermute(x, axis, [(i, i ^ 1 << stride) for i in range(lax.axis_size(axis))])


def local(grad, momentum, right_basis):
    regrouped = lax.all_to_all(grad, "cols", split_axis=1, concat_axis=0, tiled=True)
    blend = momentum + regrouped.astype(jnp.float32)
    blend_half = blend.astype(jnp.bfloat16)
    partial_panel = jnp.dot(blend_half, right_basis, preferred_element_type=jnp.float32)
    panel_total = lax.psum(partial_panel, "cols")
    gram_local = jnp.dot(panel_total.T, panel_total, precision=lax.Precision.HIGHEST)
    gram_running = gram_local
    levels = lax.axis_size("rows").bit_length() - 1
    for level in range(levels):
        partner = partner_2(gram_running, "rows", level)
        gram_running = gram_running + partner
    lower_factor = jnp.linalg.cholesky(gram_running)
    left_factor = jax.scipy.linalg.solve_triangular(lower_factor, panel_total.T, lower=True).T
    left_half = left_factor.astype(jnp.bfloat16)
    contract_rows = (((0,), (0,)), ((), ()))
    term = lax.dot_general(blend_half, left_half, contract_rows, preferred_element_type=jnp.float32)
    projected = lax.psum(term.astype(jnp.bfloat16), "rows").astype(jnp.float32)
    column_sums = lax.psum(jnp.sum(projected * projected, axis=0), "cols")
    projected_half = projected.astype(jnp.bfloat16)
    right_new = (projected / jnp.sqrt(column_sums + epsilon)).astype(jnp.bfloat16)
    contract_cols = (((1,), (1,)), ((), ()))
    feedback = lax.dot_general(
        left_half, projected_half, contract_cols, preferred_element_type=jnp.float32
    )
    momentum_new = blend - feedback_weight * feedback
    return (momentum_new, left_factor, right_new)


def solution(mesh):
    placed = (P(("rows", "cols"), None), P("rows", "cols"), P("cols", None))
    return jax.shard_map(
        local,
        mesh=mesh,
        in_specs=placed,
        out_specs=(P("rows", "cols"), P("rows", None), P("cols", None)),
        check_vma=False,
    )
```

profile of v0, /device:TPU:0, one launch (start us, length us, event | category | flops | bytes accessed | tf_op | source)
XLA Modules:
  0.0 999.2 jit_solution(17196737856015345715)
XLA Ops:
  7.2 7.5 copy.14
  14.7 324.1 %all_to_all.13 = bf16[896,4,2048]{2,0,1:T(8,128)(2,1)} all-to-all(bf16[896,4,2048]{2,0,1:T(8,128)(2,1)S(1)} %bitcast.77), channel_id=1, replica_groups=mesh['rows'=8,'cols'=4] {'cols'}, dimensions={1} | all-to-all | bytes 29360128 | tf_op jit(solution)/shard_map/all_to_all | solution.py:15
  338.8 29.8 %fusion = (bf16[3584,2048]{1,0:T(8,128)(2,1)}, f32[3584,2048]{1,0:T(8,128)}) fusion(f32[3584,2048]{1,0:T(8,128)} %param.4, bf16[896,4,2048]{2,0,1:T(8,128)(2,1)} %all_to_all.13), kind=kLoop, calls=%fused_computation.5 | loop fusion | flops 22020096 | bytes 88080384 | tf_op jit(solution)/shard_map/convert_element_type | solution.py:17
  368.6 12.9 %fusion.45 = f32[3584,512]{1,0:T(8,128)} fusion(bf16[3584,2048]{1,0:T(8,128)(2,1)} %get-tuple-element.24, bf16[2048,512]{1,0:T(8,128)(2,1)S(1)} %copy-done), kind=kOutput, calls=%fused_computation.83 | convolution fusion | flops 7516192768 | bytes 24117248 | tf_op jit(solution)/shard_map/dot_general | solution.py:18
  381.6 256.9 %all-reduce.4.cloned.1.call-done = f32[3584,512]{1,0:T(8,128)} async-done(((f32[3584,512]{1,0:T(8,128)}), f32[3584,512]{1,0:T(8,128)}) %all-reduce.4.cloned.1.call-update) | async-done | bytes 7340048 | tf_op jit(solution)/shard_map/psum | solution.py:19
  638.5 17.1 %fusion.46 = f32[512,512]{0,1:T(8,128)S(1)} fusion(f32[3584,512]{1,0:T(8,128)} %all-reduce.4.cloned.1.call-done), kind=kOutput, calls=%fused_computation.84 | convolution fusion | flops 11274289152 | bytes 8388608 | tf_op jit(solution)/shard_map/dot_general | solution.py:20
  655.6 2.6 collective-permute-done
  658.5 1.5 collective-permute-start.1
  660.0 23.7 %collective-permute-done.1 = f32[512,512]{0,1:T(8,128)S(1)} collective-permute-done((f32[512,512]{0,1:T(8,128)S(1)}, f32[512,512]{0,1:T(8,128)S(1)}, u32[]{:S(2)}, u32[]{:S(2)}) %collective-permute-start.1) | collective-permute-done | bytes 1048608 | tf_op jit(solution)/shard_map/ppermute | solution.py:11
  684.0 1.5 collective-permute-start.2
  685.5 22.9 %collective-permute-done.2 = f32[512,512]{0,1:T(8,128)S(1)} collective-permute-done((f32[512,512]{0,1:T(8,128)S(1)}, f32[512,512]{0,1:T(8,128)S(1)}, u32[]{:S(2)}, u32[]{:S(2)}) %collective-permute-start.2) | collective-permute-done | bytes 1048608 | tf_op jit(solution)/shard_map/ppermute | solution.py:11
  709.2 11.7 %cholesky.104 = f32[128,128]{1,0:T(8,128)S(1)} custom-call(f32[128,128]{1,0:T(8,128)S(1)} %cholesky.266), custom_call_target="Cholesky" | custom-call | tf_op jit(solution)/shard_map/jit(cholesky)/cholesky | solution.py:26
  720.9 9.8 custom-call.31
  731.6 11.7 %cholesky.217 = f32[128,128]{1,0:T(8,128)S(1)} custom-call(f32[128,128]{1,0:T(8,128)S(1)} %cholesky.270), custom_call_target="Cholesky" | custom-call | tf_op jit(solution)/shard_map/jit(cholesky)/cholesky | solution.py:26
  743.3 10.2 %custom-call.32 = f32[1,128,128]{1,2,0:T(8,128)S(1)} custom-call(f32[1,128,128]{2,1,0:T(8,128)S(1)} %get-tuple-element.32), custom_call_target="InvertDiagBlocksLowerTriangular" | custom-call | tf_op jit(solution)/shard_map/jit(cholesky)/cholesky | solution.py:26
  754.2 11.7 %cholesky.238 = f32[128,128]{1,0:T(8,128)S(1)} custom-call(f32[128,128]{1,0:T(8,128)S(1)} %cholesky.275), custom_call_target="Cholesky" | custom-call | tf_op jit(solution)/shard_map/jit(cholesky)/cholesky | solution.py:26
  765.9 0.7 compare_reduce_fusion.1
  766.6 9.8 custom-call.33
  776.7 0.4 slice_subtract_fusion.2
  777.0 11.9 %cholesky.255 = f32[128,128]{1,0:T(8,128)S(1)} custom-call(f32[128,128]{1,0:T(8,128)S(1)} %slice_subtract_fusion.2), custom_call_target="Cholesky" | custom-call | tf_op jit(solution)/shard_map/jit(cholesky)/cholesky | solution.py:26
  788.9 0.7 compare_reduce_fusion
  789.6 0.6 compare_reduce_fusion.2
  792.9 8.2 while.1
  793.0 0.6 fusion.59
  793.5 1.4 bitcast_dynamic-update-slice_fusion.2
  795.0 0.6 fusion.59
  795.6 1.4 bitcast_dynamic-update-slice_fusion.2
  797.1 0.6 fusion.59
  797.7 1.4 bitcast_dynamic-update-slice_fusion.2
  799.1 0.6 fusion.59
  799.7 1.4 bitcast_dynamic-update-slice_fusion.2
  801.1 39.3 %custom-call.34 = f32[4,128,128]{1,2,0:T(8,128)S(1)} custom-call(f32[4,128,128]{2,1,0:T(8,128)S(1)} %get-tuple-element.10), custom_call_target="InvertDiagBlocksLowerTriangular" | custom-call | tf_op jit(solution)/shard_map/jit(_solve_triangular)/triangular_solve | solution.py:27
  840.4 3.2 fusion.15
  843.7 5.3 convolution_subtract_fusion.1
  848.9 1.8 fusion.33
  850.7 8.8 convolution_subtract_fusion
  859.5 1.8 fusion.31
  861.3 11.4 %fusion.7 = f32[128,3584]{0,1:T(8,128)S(1)} fusion(f32[128,3584]{1,0:T(8,128)S(1)} %fusion.31, f32[128,3584]{1,0:T(8,128)S(1)} %fusion.33, f32[128,3584]{1,0:T(8,128)S(1)} %fusion.15, f32[512,3584]{0,1:T(8,128)} %bitcast.76, f32[512,512]{1,0:T(8,128)S(1)} %get-tuple-element.93), kind=kOutput, calls=%fused_computation.17 | convolution fusion | flops 2117140480 | bytes 9371648 | tf_op jit(solution)/shard_map/jit(_solve_triangular)/triangular_solve | solution.py:27
  872.7 1.9 fusion.30
  874.7 1.2 copy-done.5
  875.9 12.3 %convolution_convert_fusion = bf16[2048,512]{1,0:T(8,128)(2,1)} fusion(bf16[3584,2048]{1,0:T(8,128)(2,1)} %get-tuple-element.24, f32[128,3584]{1,0:T(8,128)S(1)} %fusion.30, f32[128,3584]{1,0:T(8,128)S(1)} %fusion.31, f32[128,3584]{1,0:T(8,128)S(1)} %fusion.33, f32[128,3584]{1,0:T(8,128)S(1)} %fusion.15), kind=kOutput, calls=%fused_computation.23 | convolution fusion | flops 7531921408 | bytes 24117248 | tf_op jit(solution)/shard_map/dot_general | solution.py:30
  888.2 5.1 maximum_bitcast_fusion
  893.3 8.4 copy.10
  901.7 47.0 %all-reduce.6.cloned.1.call-done = bf16[2048,512]{1,0:T(8,128)(2,1)} async-done(((bf16[2048,512]{1,0:T(8,128)(2,1)}), bf16[2048,512]{1,0:T(8,128)(2,1)}) %all-reduce.6.cloned.1.call-update) | async-done | bytes 2097168 | tf_op jit(solution)/shard_map/psum | solution.py:31
  948.7 2.1 fusion.10
  950.8 11.7 %psum.23 = f32[512]{0:T(512)S(1)} all-reduce(f32[512]{0:T(512)S(1)} %fusion.10), channel_id=1, replica_groups=mesh['rows'=8,'cols'=4] {'cols'}, use_global_device_ids=true, to_apply=%region_11.12 | all-reduce | flops 512 | bytes 4096 | tf_op jit(solution)/shard_map/psum | solution.py:32
  962.5 26.3 %multiply_subtract_fusion = f32[3584,2048]{1,0:T(8,128)} fusion(f32[3584,2048]{1,0:T(8,128)} %get-tuple-element.25, bf16[2048,512]{1,0:T(8,128)(2,1)} %all-reduce.6.cloned.1.call-done, f32[128,3584]{1,0:T(8,128)} %copy-done.5, f32[128,3584]{1,0:T(8,128)} %copy-done.4, f32[128,3584]{1,0:T(8,128)} %copy-done.3, f32[128,3584]{1,0:T(8,128)} %copy-done.2), kind=kOutput, calls=%fused_computation.3 | convolution fusion | flops 7545552896 | bytes 68157440 | tf_op jit(solution)/shard_map/dot_general | solution.py:36
  988.8 3.3 fusion.11
  (43 shorter events, 3.6 us)
Async XLA Ops:
  7.2 361.5 %copy-start = (bf16[2048,512]{1,0:T(8,128)(2,1)S(1)}, bf16[2048,512]{1,0:T(8,128)(2,1)}, u32[]{:S(2)}) copy-start(bf16[2048,512]{1,0:T(8,128)(2,1)} %param.5) | copy-start | bytes 6291460
  7.2 631.3 %all-reduce.4.cloned.1.call-start = ((), (), s32[]{:S(2)}) async-start(), calls=%async_computation.1 | async-start | bytes 14680064 | tf_op jit(solution)/shard_map/psum | solution.py:19
  381.6 567.1 %all-reduce.6.cloned.1.call-start = ((), (), s32[]{:S(2)}) async-start(), calls=%async_computation.2 | async-start | bytes 4194304 | tf_op jit(solution)/shard_map/psum | solution.py:31
  655.5 2.7 collective-permute-start
  658.5 25.3 %collective-permute-start.1 = (f32[512,512]{0,1:T(8,128)S(1)}, f32[512,512]{0,1:T(8,128)S(1)}, u32[]{:S(2)}, u32[]{:S(2)}) collective-permute-start(f32[512,512]{0,1:T(8,128)S(1)} %add.66), channel_id=1, source_target_pairs={{0,8},{4,12},{8,0},{12,4},{16,24},{20,28},{24,16},{28,20},{1,9},{5... | collective-permute-start | bytes 3145736 | tf_op jit(solution)/shard_map/ppermute | solution.py:11
  684.0 24.4 %collective-permute-start.2 = (f32[512,512]{0,1:T(8,128)S(1)}, f32[512,512]{0,1:T(8,128)S(1)}, u32[]{:S(2)}, u32[]{:S(2)}) collective-permute-start(f32[512,512]{0,1:T(8,128)S(1)} %add.67), channel_id=1, source_target_pairs={{0,16},{4,20},{8,24},{12,28},{16,0},{20,4},{24,8},{28,12},{1,17},{... | collective-permute-start | bytes 3145736 | tf_op jit(solution)/shard_map/ppermute | solution.py:11
  843.6 44.6 %copy-start.2 = (f32[128,3584]{1,0:T(8,128)}, f32[128,3584]{1,0:T(8,128)S(1)}, u32[]{:S(2)}) copy-start(f32[128,3584]{1,0:T(8,128)S(1)} %fusion.15) | copy-start | bytes 5505028
  850.7 23.9 %copy-start.3 = (f32[128,3584]{1,0:T(8,128)}, f32[128,3584]{1,0:T(8,128)S(1)}, u32[]{:S(2)}) copy-start(f32[128,3584]{1,0:T(8,128)S(1)} %fusion.33) | copy-start | bytes 5505028
  861.2 13.4 %copy-start.4 = (f32[128,3584]{1,0:T(8,128)}, f32[128,3584]{1,0:T(8,128)S(1)}, u32[]{:S(2)}) copy-start(f32[128,3584]{1,0:T(8,128)S(1)} %fusion.31) | copy-start | bytes 5505028
  874.7 1.2 copy-start.5
  962.5 29.6 %copy-start.1 = (bf16[2048,512]{1,0:T(8,128)(2,1)S(1)}, bf16[2048,512]{1,0:T(8,128)(2,1)}, u32[]{:S(2)}) copy-start(bf16[2048,512]{1,0:T(8,128)(2,1)} %param.5) | copy-start | bytes 6291460
Sparse Core Ops, SparseCore 0:
  381.7 256.7 all-reduce.3
  888.3 60.3 all-reduce.5
where the time goes:
time: 1010 us; the launch traced here: 999 us
  waiting for transfers between devices  353 us (35%)
  blocking collectives  336 us (33%)
  other arithmetic  160 us (16%)
  matrix products  105 us (10%)
  local copies, waits for them, and re-layouts  25.8 us (3%)
  between operations  17 us (2%)
    all_to_all x1, blocking collectives, local(): lax.all_to_all(grad, 'cols', split_axis=1, concat_axis=0, tiled=True)  324 us
    psum x1, waiting for transfers between devices, local(): panel_total = lax.psum(partial_panel, 'cols')  257 us
    another operation x14, other arithmetic, local(): lower_factor = jnp.linalg.cholesky(gram_running)  79 us
    ppermute x3, waiting for transfers between devices, partner_2(): lax.ppermute(x, axis, [(i, i ^ 1 << stride) for i in range(lax.axis_size(...  49.3 us
    psum x1, waiting for transfers between devices, local(): projected = lax.psum(term.astype(jnp.bfloat16), 'rows').astype(jnp.float32)  47 us
    another operation x3, other arithmetic, local(): jax.scipy.linalg.solve_triangular(lower_factor, panel_total.T, lower=True)  39.4 us
    another operation x7, matrix products, local(): jax.scipy.linalg.solve_triangular(lower_factor, panel_total.T, lower=True)  34.1 us
    convert_element_type x1, other arithmetic, local(): blend_half = blend.astype(jnp.bfloat16)  29.8 us
  transfers between devices with their start and end apart: 5, of which 5 were waited for; matrix products, arithmetic and copies ran while one was open for 1% of the time, Pallas kernels for 0%

commit v1 on v0

v1 whole, which is shorter than its diff:
```python
import jax
import jax.numpy as jnp
from jax import lax
from jax.sharding import PartitionSpec as P

epsilon = 1e-06
feedback_weight = 0.05


def shift(x, s):
    n = lax.axis_size("cols")
    return lax.ppermute(x, "cols", [(i, (i + s) % n) for i in range(n)])


def flip(x, axis, stride):
    return lax.ppermute(x, axis, [(i, i ^ stride) for i in range(lax.axis_size(axis))])


def sum_everywhere(x):
    levels = lax.axis_size("rows").bit_length() - 1
    index = lax.axis_index("rows")
    for level in range(levels):
        bit = (index >> level) & 1
        half = x.shape[0] // 2
        keep = lax.dynamic_slice_in_dim(x, bit * half, half)
        send = lax.dynamic_slice_in_dim(x, (1 - bit) * half, half)
        x = keep + flip(send, "rows", 1 << level)
    for level in range(lax.axis_size("cols").bit_length() - 1):
        x = x + flip(x, "cols", 1 << level)
    for level in reversed(range(levels)):
        bit = (index >> level) & 1
        other = flip(x, "rows", 1 << level)
        low = jnp.where(bit == 0, x, other)
        high = jnp.where(bit == 0, other, x)
        x = jnp.concatenate([low, high], axis=0)
    return x


def local(grad, momentum, right_basis):
    n = lax.axis_size("cols")
    me = lax.axis_index("cols")
    deep = grad.shape[0]
    width = momentum.shape[1]
    order = sorted(range(1, n), key=lambda s: -min(s, n - s))
    tile = lambda c: lax.dynamic_slice(grad, (0, c * width), (deep, width))
    pieces = {0: tile(me)}
    for s in order:
        pieces[s] = shift(tile((me + s) % n), s)
    regrouped = jnp.zeros((n * deep, width), grad.dtype)
    blend_half = jnp.zeros((n * deep, width), jnp.bfloat16)
    panel_own = None
    for s in [0] + order:
        source = (me - s + n) % n
        chunk = lax.dynamic_slice_in_dim(momentum, source * deep, deep) + pieces[s].astype(jnp.float32)
        chunk = chunk.astype(jnp.bfloat16)
        partial = jnp.dot(chunk, right_basis, preferred_element_type=jnp.float32)
        regrouped = lax.dynamic_update_slice_in_dim(regrouped, pieces[s], source * deep, 0)
        blend_half = lax.dynamic_update_slice_in_dim(blend_half, chunk, source * deep, 0)
        if s == 0:
            panel_own = partial
        else:
            panel_own = panel_own + shift(partial.astype(jnp.bfloat16), -s).astype(jnp.float32)
    gram = sum_everywhere(jnp.dot(panel_own.T, panel_own, precision=lax.Precision.HIGHEST))
    panel = jnp.zeros((n * deep, panel_own.shape[1]), jnp.float32)
    panel = lax.dynamic_update_slice_in_dim(panel, panel_own, me * deep, 0)
    for s in range(1, n):
        panel = lax.dynamic_update_slice_in_dim(panel, shift(panel_own, s), (me - s + n) % n * deep, 0)
    lower_factor = jnp.linalg.cholesky(gram)
    left_factor = jax.scipy.linalg.solve_triangular(lower_factor, panel.T, lower=True).T
    left_half = left_factor.astype(jnp.bfloat16)
    contract_rows = (((0,), (0,)), ((), ()))
    term = lax.dot_general(blend_half, left_half, contract_rows, preferred_element_type=jnp.float32)
    projected = lax.psum(term.astype(jnp.bfloat16), "rows").astype(jnp.float32)
    column_sums = lax.psum(jnp.sum(projected * projected, axis=0), "cols")
    projected_half = projected.astype(jnp.bfloat16)
    right_new = (projected / jnp.sqrt(column_sums + epsilon)).astype(jnp.bfloat16)
    contract_cols = (((1,), (1,)), ((), ()))
    feedback = lax.dot_general(
        left_half, projected_half, contract_cols, preferred_element_type=jnp.float32
    )
    blend = momentum + regrouped.astype(jnp.float32)
    momentum_new = blend - feedback_weight * feedback
    return (momentum_new, left_factor, right_new)


def solution(mesh):
    placed = (P(("rows", "cols"), None), P("rows", "cols"), P("cols", None))
    return jax.shard_map(
        local,
        mesh=mesh,
        in_specs=placed,
        out_specs=(P("rows", "cols"), P("rows", None), P("cols", None)),
        check_vma=False,
    )
```

time: 1010 us -> 948 us (0.939)
  blocking collectives: 336 us -> 11.7 us
  starting transfers between devices: 3.23 us -> 196 us
  waiting for transfers between devices: 353 us -> 387 us
  other arithmetic: 160 us -> 181 us
  local copies, waits for them, and re-layouts: 25.8 us -> 46.3 us
    all_to_all x1 -> x0, blocking collectives: 324 us -> none  [local(): lax.all_to_all(grad, 'cols', split_axis=1, concat_axis=0, tiled=True)]
    psum x1 -> x0, waiting for transfers between devices: 257 us -> none  [local(): panel_total = lax.psum(partial_panel, 'cols')]
    ppermute x3 -> x17, waiting for transfers between devices: 49.3 us -> 304 us  [the longest x9 282 us: shift(): return lax.ppermute(x, 'cols', [(i, (i + s) % n) for i in range(n)])]
    ppermute x3 -> x17, starting transfers between devices: 3.15 us -> 195 us  [the longest x9 188 us: shift(): return lax.ppermute(x, 'cols', [(i, (i + s) % n) for i in range(n)])]
    dynamic_update_slice x0 -> x5, other arithmetic: none -> 49.3 us  [the longest x4 46 us: local(): lax.dynamic_update_slice_in_dim(blend_half, chunk, source * deep, 0)]
    psum x1, waiting for transfers between devices: 47 us -> 82.9 us  [local(): projected = lax.psum(term.astype(jnp.bfloat16), 'rows').astype(jnp.float32)]
    convert_element_type x1 -> x0, other arithmetic: 29.8 us -> none  [local(): blend_half = blend.astype(jnp.bfloat16)]
    another operation x17 -> x19, local copies, waits for them, and re-layouts: 8.28 us -> 22.2 us
  transfers between devices with their start and end apart: 5 -> 18, of which waited for: 5 -> 10; matrix products, arithmetic and copies ran while one was open for 1% -> 9% of each run, Pallas kernels for 0% -> 0%
where the time goes in v1:
time: 948 us; the launch traced here: 943 us
  waiting for transfers between devices  387 us (41%)
  starting transfers between devices  196 us (21%)
  other arithmetic  181 us (19%)
  matrix products  103 us (11%)
  local copies, waits for them, and re-layouts  46.3 us (5%)
  between operations  17.2 us (2%)
  blocking collectives  11.7 us (1%)
    ppermute x9, waiting for transfers between devices, shift(): return lax.ppermute(x, 'cols', [(i, (i + s) % n) for i in range(n)])  282 us
    ppermute x9, starting transfers between devices, shift(): return lax.ppermute(x, 'cols', [(i, (i + s) % n) for i in range(n)])  188 us
    psum x1, waiting for transfers between devices, local(): projected = lax.psum(term.astype(jnp.bfloat16), 'rows').astype(jnp.float32)  82.9 us
    another operation x14, other arithmetic, local(): lower_factor = jnp.linalg.cholesky(gram)  79 us
    dynamic_update_slice x4, other arithmetic, local(): lax.dynamic_update_slice_in_dim(blend_half, chunk, source * deep, 0)  46 us
    another operation x3, other arithmetic, local(): jax.scipy.linalg.solve_triangular(lower_factor, panel.T, lower=True)  39.4 us
    another operation x7, matrix products, local(): jax.scipy.linalg.solve_triangular(lower_factor, panel.T, lower=True)  32.2 us
    dot_general x1, matrix products, local(): lax.dot_general(left_half, projected_half, contract_cols, preferred_eleme...  27.9 us
  transfers between devices with their start and end apart: 18, of which 10 were waited for; matrix products, arithmetic and copies ran while one was open for 9% of the time, Pallas kernels for 0%

profile of v1, /device:TPU:0, one launch (start us, length us, event | category | flops | bytes accessed | tf_op | source)
XLA Modules:
  0.0 942.6 jit_solution(13194718705285914622)
XLA Ops:
  7.3 7.3 broadcast.196.clone
  14.6 14.9 %constant_dynamic-update-slice_fusion.3 = (bf16[3584,2048]{1,0:T(8,128)(2,1)}, bf16[896,2048]{1,0:T(8,128)(2,1)}, bf16[896,2048]{1,0:T(8,128)(2,1)}, bf16[896,2048]{1,0:T(8,128)(2,1)}, bf16[896,2048]{1,0:T(8,128)(2,1)}) fusion(bf16[3584,2048]{1,0:T(8,128)(2,1)} %broadcast.196.clone, s32[]{:T(128)S(6)} %select_n.129, bf16[896,8192]{1,0:T(8,128)(2,1)} %param.3, ...), kind=kLoop, calls=%fused_computation.90 | loop fusion | flops 5505024 | bytes 40370196 | tf_op jit(solution)/shard_map/dynamic_update_slice | solution.py:58
  29.5 5.0 collective-permute-start.2
  35.6 79.0 %collective-permute-done.2 = bf16[896,2048]{1,0:T(8,128)(2,1)} collective-permute-done((bf16[896,2048]{1,0:T(8,128)(2,1)}, bf16[896,2048]{1,0:T(8,128)(2,1)}, u32[]{:S(2)}, u32[]{:S(2)}) %collective-permute-start.2) | collective-permute-done | bytes 3670048 | tf_op jit(solution)/shard_map/ppermute | solution.py:12
  114.6 7.2 convolution_convert_fusion.1
  121.8 176.4 %collective-permute-start.5 = (bf16[896,512]{1,0:T(8,128)(2,1)}, bf16[896,512]{1,0:T(8,128)(2,1)S(1)}, u32[]{:S(2)}, u32[]{:S(2)}) collective-permute-start(bf16[896,512]{1,0:T(8,128)(2,1)} %convolution_convert_fusion.1), channel_id=1, source_target_pairs={{0,1},{1,2},{2,3},{3,0},{4,5},{5,6},{6,7},{7,4},{8,9},{9,10},{10,1... | collective-permute-start | bytes 2752520 | tf_op jit(solution)/shard_map/ppermute | solution.py:12
  298.2 7.2 convolution_convert_fusion.2
  305.8 64.3 %collective-permute-done = bf16[896,2048]{1,0:T(8,128)(2,1)} collective-permute-done((bf16[896,2048]{1,0:T(8,128)(2,1)}, bf16[896,2048]{1,0:T(8,128)(2,1)}, u32[]{:S(2)}, u32[]{:S(2)}) %collective-permute-start) | collective-permute-done | bytes 3670048 | tf_op jit(solution)/shard_map/ppermute | solution.py:12
  370.1 7.3 convolution_convert_fusion.3
  377.4 4.1 fusion.38
  381.5 46.5 %collective-permute-done.3 = bf16[896,512]{1,0:T(8,128)(2,1)} collective-permute-done((bf16[896,512]{1,0:T(8,128)(2,1)}, bf16[896,512]{1,0:T(8,128)(2,1)}, u32[]{:S(2)}, u32[]{:S(2)}) %collective-permute-start.3) | collective-permute-done | bytes 917536 | tf_op jit(solution)/shard_map/ppermute | solution.py:12
  428.0 4.0 broadcast_in_dim.6
  432.0 3.3 constant_dynamic-update-slice_fusion.7
  435.3 3.5 fusion.39
  439.7 2.2 collective-permute-done.6
  445.4 6.9 collective-permute-done.7
  455.0 6.0 collective-permute-done.8
  461.2 6.6 collective-permute-done.9
  469.4 7.1 broadcast.196.clone.1
  476.5 4.3 dynamic-slice_dynamic-update-slice_fusion
  482.4 10.4 %constant_dynamic-update-slice_fusion.2 = (bf16[3584,2048]{1,0:T(8,128)(2,1)}, bf16[3584,2048]{1,0:T(8,128)(2,1)}) fusion(bf16[3584,2048]{1,0:T(8,128)(2,1)} %get-tuple-element.24, s32[]{:T(128)S(6)} %select_n.132, bf16[896,2048]{1,0:T(8,128)(2,1)} %collective-permute-done, f32[3584,2048]{1,0:T(8,128)} %param.4, ...), kind=kLoop, calls=%fused_computation.89 | loop fusion | flops 5505024 | bytes 18350084 | tf_op jit(solution)/shard_map/dynamic_update_slice | solution.py:58
  499.2 10.4 %constant_dynamic-update-slice_fusion.1 = (bf16[3584,2048]{1,0:T(8,128)(2,1)}, bf16[3584,2048]{1,0:T(8,128)(2,1)}) fusion(bf16[3584,2048]{1,0:T(8,128)(2,1)} %get-tuple-element.35, s32[]{:T(128)S(6)} %select_n.136, bf16[896,2048]{1,0:T(8,128)(2,1)} %collective-permute-done.1, f32[3584,2048]{1,0:T(8,128)} %param.4, bf16[3584,2048]{1,0:T(8,128)(2,1)} %get-tuple-element.36), kind=kLoop, calls=%fused_computation.88 | loop fusion | flops 5505024 | bytes 18350084 | tf_op jit(solution)/shard_map/dynamic_update_slice | solution.py:58
  509.9 10.4 %constant_dynamic-update-slice_fusion = (bf16[3584,2048]{1,0:T(8,128)(2,1)}, bf16[3584,2048]{1,0:T(8,128)(2,1)}) fusion(bf16[3584,2048]{1,0:T(8,128)(2,1)} %get-tuple-element.33, s32[]{:T(128)S(6)} %select_n.138, bf16[896,2048]{1,0:T(8,128)(2,1)} %collective-permute-done.2, f32[3584,2048]{1,0:T(8,128)} %param.4, bf16[3584,2048]{1,0:T(8,128)(2,1)} %get-tuple-element.34), kind=kLoop, calls=%fused_computation.87 | loop fusion | flops 5505024 | bytes 18350084 | tf_op jit(solution)/shard_map/dynamic_update_slice | solution.py:58
  520.2 17.4 %collective-permute-done.14 = f32[896,512]{1,0:T(8,128)S(1)} collective-permute-done((f32[896,512]{1,0:T(8,128)S(1)}, f32[896,512]{1,0:T(8,128)S(1)}, u32[]{:S(2)}, u32[]{:S(2)}) %collective-permute-start.14) | collective-permute-done | bytes 1835040 | tf_op jit(solution)/shard_map/ppermute | solution.py:12
  539.0 75.1 %collective-permute-done.15 = f32[896,512]{1,0:T(8,128)S(1)} collective-permute-done((f32[896,512]{1,0:T(8,128)S(1)}, f32[896,512]{1,0:T(8,128)S(1)}, u32[]{:S(2)}, u32[]{:S(2)}) %collective-permute-start.15) | collective-permute-done | bytes 1835040 | tf_op jit(solution)/shard_map/ppermute | solution.py:12
  617.6 11.7 %cholesky.104 = f32[128,128]{1,0:T(8,128)S(1)} custom-call(f32[128,128]{1,0:T(8,128)S(1)} %cholesky.266), custom_call_target="Cholesky" | custom-call | tf_op jit(solution)/shard_map/jit(cholesky)/cholesky | solution.py:68
  629.5 9.8 %custom-call.31 = f32[1,128,128]{1,2,0:T(8,128)S(1)} custom-call(f32[1,128,128]{2,1,0:T(8,128)S(1)} %get-tuple-element.52), custom_call_target="InvertDiagBlocksLowerTriangular" | custom-call | tf_op jit(solution)/shard_map/jit(cholesky)/cholesky | solution.py:68
  640.0 12.1 %cholesky.217 = f32[128,128]{1,0:T(8,128)S(1)} custom-call(f32[128,128]{1,0:T(8,128)S(1)} %cholesky.270), custom_call_target="Cholesky" | custom-call | tf_op jit(solution)/shard_map/jit(cholesky)/cholesky | solution.py:68
  652.1 9.8 %custom-call.32 = f32[1,128,128]{1,2,0:T(8,128)S(1)} custom-call(f32[1,128,128]{2,1,0:T(8,128)S(1)} %get-tuple-element.49), custom_call_target="InvertDiagBlocksLowerTriangular" | custom-call | tf_op jit(solution)/shard_map/jit(cholesky)/cholesky | solution.py:68
  662.6 11.7 %cholesky.238 = f32[128,128]{1,0:T(8,128)S(1)} custom-call(f32[128,128]{1,0:T(8,128)S(1)} %cholesky.275), custom_call_target="Cholesky" | custom-call | tf_op jit(solution)/shard_map/jit(cholesky)/cholesky | solution.py:68
  674.4 9.8 %custom-call.33 = f32[1,128,128]{1,2,0:T(8,128)S(1)} custom-call(f32[1,128,128]{2,1,0:T(8,128)S(1)} %get-tuple-element.46), custom_call_target="InvertDiagBlocksLowerTriangular" | custom-call | tf_op jit(solution)/shard_map/jit(cholesky)/cholesky | solution.py:68
  684.8 11.9 %cholesky.255 = f32[128,128]{1,0:T(8,128)S(1)} custom-call(f32[128,128]{1,0:T(8,128)S(1)} %convolution_subtract_fusion.2), custom_call_target="Cholesky" | custom-call | tf_op jit(solution)/shard_map/jit(cholesky)/cholesky | solution.py:68
  701.4 7.7 while.1
  709.1 39.3 %custom-call.34 = f32[4,128,128]{1,2,0:T(8,128)S(1)} custom-call(f32[4,128,128]{2,1,0:T(8,128)S(1)} %get-tuple-element.10), custom_call_target="InvertDiagBlocksLowerTriangular" | custom-call | tf_op jit(solution)/shard_map/jit(_solve_triangular)/triangular_solve | solution.py:69
  748.4 3.2 fusion.15
  751.7 3.1 fusion.28
  754.8 3.3 fusion.14
  758.1 6.6 fusion.8
  764.7 3.3 fusion.13
  768.0 9.2 fusion
  777.2 3.5 fusion.12
  782.0 12.3 %convolution_convert_fusion = bf16[2048,512]{1,0:T(8,128)(2,1)} fusion(bf16[3584,2048]{1,0:T(8,128)(2,1)} %get-tuple-element.31, f32[128,3584]{1,0:T(8,128)S(1)} %fusion.12, f32[128,3584]{1,0:T(8,128)S(1)} %fusion.13, f32[128,3584]{1,0:T(8,128)S(1)} %fusion.14, f32[128,3584]{1,0:T(8,128)S(1)} %fusion.15), kind=kOutput, calls=%fused_computation.23 | convolution fusion | flops 7531921408 | bytes 24117248 | tf_op jit(solution)/shard_map/dot_general | solution.py:72
  794.3 5.1 maximum_bitcast_fusion
  799.3 8.4 copy.9
  807.7 82.9 %all-reduce.3.cloned.1.call-done = bf16[2048,512]{1,0:T(8,128)(2,1)} async-done(((bf16[2048,512]{1,0:T(8,128)(2,1)}), bf16[2048,512]{1,0:T(8,128)(2,1)}) %all-reduce.3.cloned.1.call-update) | async-done | bytes 2097168 | tf_op jit(solution)/shard_map/psum | solution.py:73
  892.7 11.7 %psum.15 = f32[512]{0:T(512)S(1)} all-reduce(f32[512]{0:T(512)S(1)} %fusion.6), channel_id=1, replica_groups=mesh['rows'=8,'cols'=4] {'cols'}, use_global_device_ids=true, to_apply=%region_10.11 | all-reduce | flops 512 | bytes 4096 | tf_op jit(solution)/shard_map/psum | solution.py:74
  904.4 27.9 %multiply_subtract_fusion = f32[3584,2048]{1,0:T(8,128)} fusion(f32[3584,2048]{1,0:T(8,128)} %param.4, bf16[3584,2048]{1,0:T(8,128)(2,1)} %get-tuple-element.32, bf16[2048,512]{1,0:T(8,128)(2,1)} %all-reduce.3.cloned.1.call-done, f32[128,3584]{1,0:T(8,128)} %copy-done.5, f32[128,3584]{1,0:T(8,128)} %copy-done.4, f32[128,3584]{1,0:T(8,128)} %copy-done.3, ...), kind=kOutput, calls=%fused_computation.2 | convolution fusion | flops 7560232960 | bytes 82837504 | tf_op jit(solution)/shard_map/dot_general | solution.py:78
  932.3 3.3 fusion.7
  (93 shorter events, 38.7 us)
Async XLA Ops:
  7.2 107.4 %copy-start = (bf16[2048,512]{1,0:T(8,128)(2,1)S(1)}, bf16[2048,512]{1,0:T(8,128)(2,1)}, u32[]{:S(2)}) copy-start(bf16[2048,512]{1,0:T(8,128)(2,1)} %param.5) | copy-start | bytes 6291460
  7.2 883.4 %all-reduce.3.cloned.1.call-start = ((), (), s32[]{:S(2)}) async-start(), calls=%async_computation | async-start | bytes 4194304 | tf_op jit(solution)/shard_map/psum | solution.py:73
  29.5 85.1 %collective-permute-start.2 = (bf16[896,2048]{1,0:T(8,128)(2,1)}, bf16[896,2048]{1,0:T(8,128)(2,1)}, u32[]{:S(2)}, u32[]{:S(2)}) collective-permute-start(bf16[896,2048]{1,0:T(8,128)(2,1)} %get-tuple-element.29), channel_id=1, source_target_pairs={{0,3},{1,0},{2,1},{3,2},{4,7},{5,4},{6,5},{7,6},{8,11},{9,8},{10,9... | collective-permute-start | bytes 11010056 | tf_op jit(solution)/shard_map/ppermute | solution.py:12
  34.5 263.6 %collective-permute-start.1 = (bf16[896,2048]{1,0:T(8,128)(2,1)}, bf16[896,2048]{1,0:T(8,128)(2,1)}, u32[]{:S(2)}, u32[]{:S(2)}) collective-permute-start(bf16[896,2048]{1,0:T(8,128)(2,1)} %get-tuple-element.30), channel_id=1, source_target_pairs={{0,1},{1,2},{2,3},{3,0},{4,5},{5,6},{6,7},{7,4},{8,9},{9,10},{10,1... | collective-permute-start | bytes 11010056 | tf_op jit(solution)/shard_map/ppermute | solution.py:12
  34.5 335.6 %collective-permute-start = (bf16[896,2048]{1,0:T(8,128)(2,1)}, bf16[896,2048]{1,0:T(8,128)(2,1)}, u32[]{:S(2)}, u32[]{:S(2)}) collective-permute-start(bf16[896,2048]{1,0:T(8,128)(2,1)} %get-tuple-element.28), channel_id=1, source_target_pairs={{0,2},{1,3},{2,0},{3,1},{4,6},{5,7},{6,4},{7,5},{8,10},{9,11},{10,... | collective-permute-start | bytes 11010056 | tf_op jit(solution)/shard_map/ppermute | solution.py:12
  121.8 259.7 %collective-permute-start.5 = (bf16[896,512]{1,0:T(8,128)(2,1)}, bf16[896,512]{1,0:T(8,128)(2,1)S(1)}, u32[]{:S(2)}, u32[]{:S(2)}) collective-permute-start(bf16[896,512]{1,0:T(8,128)(2,1)} %convolution_convert_fusion.1), channel_id=1, source_target_pairs={{0,1},{1,2},{2,3},{3,0},{4,5},{5,6},{6,7},{7,4},{8,9},{9,10},{10,1... | collective-permute-start | bytes 2752520 | tf_op jit(solution)/shard_map/ppermute | solution.py:12
  305.4 76.1 %collective-permute-start.4 = (bf16[896,512]{1,0:T(8,128)(2,1)}, bf16[896,512]{1,0:T(8,128)(2,1)}, u32[]{:S(2)}, u32[]{:S(2)}) collective-permute-start(bf16[896,512]{1,0:T(8,128)(2,1)} %convolution_convert_fusion.2), channel_id=1, source_target_pairs={{0,3},{1,0},{2,1},{3,2},{4,7},{5,4},{6,5},{7,6},{8,11},{9,8},{10,9... | collective-permute-start | bytes 2752520 | tf_op jit(solution)/shard_map/ppermute | solution.py:12
  377.4 50.6 %collective-permute-start.3 = (bf16[896,512]{1,0:T(8,128)(2,1)}, bf16[896,512]{1,0:T(8,128)(2,1)}, u32[]{:S(2)}, u32[]{:S(2)}) collective-permute-start(bf16[896,512]{1,0:T(8,128)(2,1)} %convolution_convert_fusion.3), channel_id=1, source_target_pairs={{0,2},{1,3},{2,0},{3,1},{4,6},{5,7},{6,4},{7,5},{8,10},{9,11},{10,... | collective-permute-start | bytes 2752520 | tf_op jit(solution)/shard_map/ppermute | solution.py:12
  439.7 2.3 collective-permute-start.6
  443.0 0.8 copy-start.6
  443.9 8.4 collective-permute-start.7
  453.4 7.6 collective-permute-start.8
  461.2 6.7 collective-permute-start.9
  467.9 12.9 %collective-permute-start.10 = (f32[64,512]{0,1:T(8,128)S(1)}, f32[64,512]{0,1:T(8,128)S(1)}, u32[]{:S(2)}, u32[]{:S(2)}) collective-permute-start(f32[64,512]{0,1:T(8,128)S(1)} %add.225), channel_id=1, source_target_pairs={{0,2},{1,3},{2,0},{3,1},{4,6},{5,7},{6,4},{7,5},{8,10},{9,11},{10,... | collective-permute-start | bytes 393224 | tf_op jit(solution)/shard_map/ppermute | solution.py:16
  480.8 16.6 %collective-permute-start.11 = (f32[64,512]{0,1:T(8,128)S(1)}, f32[64,512]{0,1:T(8,128)S(1)}, u32[]{:S(2)}, u32[]{:S(2)}) collective-permute-start(f32[64,512]{0,1:T(8,128)S(1)} %add.226), channel_id=1, source_target_pairs={{0,16},{4,20},{8,24},{12,28},{16,0},{20,4},{24,8},{28,12},{1,17},{... | collective-permute-start | bytes 393224 | tf_op jit(solution)/shard_map/ppermute | solution.py:16
  492.8 44.8 %collective-permute-start.14 = (f32[896,512]{1,0:T(8,128)S(1)}, f32[896,512]{1,0:T(8,128)S(1)}, u32[]{:S(2)}, u32[]{:S(2)}) collective-permute-start(f32[896,512]{1,0:T(8,128)S(1)} %get-tuple-element.23), channel_id=1, source_target_pairs={{0,1},{1,2},{2,3},{3,0},{4,5},{5,6},{6,7},{7,4},{8,9},{9,10},{10,1... | collective-permute-start | bytes 5505032 | tf_op jit(solution)/shard_map/ppermute | solution.py:12
  494.5 119.6 %collective-permute-start.15 = (f32[896,512]{1,0:T(8,128)S(1)}, f32[896,512]{1,0:T(8,128)S(1)}, u32[]{:S(2)}, u32[]{:S(2)}) collective-permute-start(f32[896,512]{1,0:T(8,128)S(1)} %get-tuple-element.23), channel_id=1, source_target_pairs={{0,2},{1,3},{2,0},{3,1},{4,6},{5,7},{6,4},{7,5},{8,10},{9,11},{10,... | collective-permute-start | bytes 5505032 | tf_op jit(solution)/shard_map/ppermute | solution.py:12
  495.3 120.2 %collective-permute-start.16 = (f32[896,512]{1,0:T(8,128)S(1)}, f32[896,512]{1,0:T(8,128)S(1)}, u32[]{:S(2)}, u32[]{:S(2)}) collective-permute-start(f32[896,512]{1,0:T(8,128)S(1)} %get-tuple-element.23), channel_id=1, source_target_pairs={{0,3},{1,0},{2,1},{3,2},{4,7},{5,4},{6,5},{7,6},{8,11},{9,8},{10,9... | collective-permute-start | bytes 5505032 | tf_op jit(solution)/shard_map/ppermute | solution.py:12
  497.7 11.9 %collective-permute-start.12 = (f32[128,512]{0,1:T(8,128)S(1)}, f32[128,512]{0,1:T(8,128)S(1)}, u32[]{:S(2)}, u32[]{:S(2)}) collective-permute-start(f32[128,512]{0,1:T(8,128)S(1)} %pad_maximum_fusion.2), channel_id=1, source_target_pairs={{0,8},{4,12},{8,0},{12,4},{16,24},{20,28},{24,16},{28,20},{1,9},{5... | collective-permute-start | bytes 786440 | tf_op jit(solution)/shard_map/ppermute | solution.py:16
  509.8 107.1 %collective-permute-start.13 = (f32[256,512]{0,1:T(8,128)S(1)}, f32[256,512]{0,1:T(8,128)S(1)}, u32[]{:S(2)}, u32[]{:S(2)}) collective-permute-start(f32[256,512]{0,1:T(8,128)S(1)} %pad_maximum_fusion.1), channel_id=1, source_target_pairs={{0,4},{4,0},{8,12},{12,8},{16,20},{20,16},{24,28},{28,24},{1,5},{5... | collective-permute-start | bytes 1572872 | tf_op jit(solution)/shard_map/ppermute | solution.py:16
  751.7 42.6 %copy-start.2 = (f32[128,3584]{1,0:T(8,128)}, f32[128,3584]{1,0:T(8,128)S(1)}, u32[]{:S(2)}) copy-start(f32[128,3584]{1,0:T(8,128)S(1)} %fusion.15) | copy-start | bytes 5505028
  758.1 22.6 %copy-start.3 = (f32[128,3584]{1,0:T(8,128)}, f32[128,3584]{1,0:T(8,128)S(1)}, u32[]{:S(2)}) copy-start(f32[128,3584]{1,0:T(8,128)S(1)} %fusion.14) | copy-start | bytes 5505028
  768.0 12.7 %copy-start.4 = (f32[128,3584]{1,0:T(8,128)}, f32[128,3584]{1,0:T(8,128)S(1)}, u32[]{:S(2)}) copy-start(f32[128,3584]{1,0:T(8,128)S(1)} %fusion.13) | copy-start | bytes 5505028
  780.7 1.3 copy-start.5
  904.4 31.2 %copy-start.1 = (bf16[2048,512]{1,0:T(8,128)(2,1)S(1)}, bf16[2048,512]{1,0:T(8,128)(2,1)}, u32[]{:S(2)}) copy-start(bf16[2048,512]{1,0:T(8,128)(2,1)} %param.5) | copy-start | bytes 6291460
Sparse Core Ops, SparseCore 0:
  794.4 96.1 all-reduce.2

commit v2 on v1

--- a/solution.py
+++ b/solution.py
@@ -1,10 +1,98 @@
 import jax
 import jax.numpy as jnp
 from jax import lax
+from jax.experimental import pallas as pl
+from jax.experimental.pallas import tpu as pltpu
 from jax.sharding import PartitionSpec as P
 
 epsilon = 1e-06
 feedback_weight = 0.05
+
+
+BLOCK = 128
+HIGHEST = lax.Precision.HIGHEST
+
+
+def rows_with(x, y, dims):
+    return lax.dot_general(x, y, (dims, ((), ())), precision=HIGHEST, preferred_element_type=jnp.float32)
+
+
+def factor_block(tile):
+    lane = lax.broadcasted_iota(jnp.int32, (8, BLOCK), 1)
+    row = lax.broadcasted_iota(jnp.int32, (8, 2 * BLOCK), 0)
+    row_half = row[:, :BLOCK]
+
+    def group(g, carry):
+        base = pl.multiple_of(g * 8, 8)
+        block = tile[pl.ds(base, 8), :]
+        left = block[:, :BLOCK]
+        columns = [
+            jnp.broadcast_to(jnp.sum(jnp.where(lane == base + j, left, 0.0), axis=1, keepdims=True), (8, BLOCK))
+            for j in range(8)
+        ]
+        for i in range(8):
+            pivot = columns[i][i:i + 1, :]
+            scale = lax.rsqrt(pivot)
+            scale = scale * (1.5 - 0.5 * pivot * scale * scale)
+            multiplier = columns[i] * scale
+            wide = jnp.concatenate([multiplier, multiplier], axis=1)
+            wide_scale = jnp.concatenate([scale, scale], axis=1)
+            top = block[i:i + 1, :] * wide_scale
+            block = jnp.where(row > i, block - wide * top, jnp.where(row == i, top, block))
+            for j in range(i + 1, 8):
+                head = columns[j][i:i + 1, :] * scale
+                columns[j] = jnp.where(row_half > i, columns[j] - multiplier * head, columns[j])
+        tile[pl.ds(base, 8), :] = block
+        below = jnp.where(lane >= base + 8, block[:, :BLOCK], 0.0).T
+        change = below[:, 0:1] * block[0:1, :]
+        for i in range(1, 8):
+            change = change + below[:, i:i + 1] * block[i:i + 1, :]
+        tile[...] = tile[...] - change
+        return carry
+
+    lax.fori_loop(0, BLOCK // 8, group, 0)
+
+
+def inverse_factor_kernel(gram_ref, out_ref, work, tile):
+    size = gram_ref.shape[0]
+    work[...] = gram_ref[...]
+    out_ref[...] = jnp.zeros_like(out_ref)
+    diagonal = lax.broadcasted_iota(jnp.int32, (BLOCK, BLOCK), 0) == lax.broadcasted_iota(jnp.int32, (BLOCK, BLOCK), 1)
+    for first in range(0, size, BLOCK):
+        last = first + BLOCK
+        tile[:, :BLOCK] = work[first:last, first:last]
+        tile[:, BLOCK:] = jnp.where(diagonal, 1.0, 0.0)
+        factor_block(tile)
+        inverse = tile[:, BLOCK:]
+        out_ref[first:last, first:last] = inverse
+        if first > 0:
+            out_ref[first:last, :first] = rows_with(inverse, out_ref[first:last, :first], ((1,), (0,)))
+        if last < size:
+            upper = rows_with(inverse, work[first:last, last:], ((1,), (0,)))
+            work[last:, last:] = work[last:, last:] - rows_with(upper, upper, ((0,), (0,)))
+            done = out_ref[first:last, :last]
+            out_ref[last:, :last] = out_ref[last:, :last] - rows_with(upper, done, ((0,), (0,)))
+
+
+def inverse_factor(gram):
+    size = gram.shape[0]
+    return pl.pallas_call(
+        inverse_factor_kernel,
+        out_shape=jax.ShapeDtypeStruct((size, size), jnp.float32),
+        in_specs=[pl.BlockSpec(memory_space=pltpu.VMEM)],
+        out_specs=pl.BlockSpec(memory_space=pltpu.VMEM),
+        scratch_shapes=[pltpu.VMEM((size, size), jnp.float32), pltpu.VMEM((BLOCK, 2 * BLOCK), jnp.float32)],
+        compiler_params=pltpu.CompilerParams(vmem_limit_bytes=16 << 20),
+        cost_estimate=pl.CostEstimate(flops=80 * 10 ** 9, bytes_accessed=2 * 4 * size * size, transcendentals=0),
+    )(gram)
+
+
+def fresh(shape, dtype):
+    return pl.pallas_call(
+        lambda out_ref: None,
+        out_shape=jax.ShapeDtypeStruct(shape, dtype),
+        out_specs=pl.BlockSpec(memory_space=pl.ANY),
+    )()
 
 
 def shift(x, s):
@@ -43,11 +131,12 @@
     width = momentum.shape[1]
     order = sorted(range(1, n), key=lambda s: -min(s, n - s))
     tile = lambda c: lax.dynamic_slice(grad, (0, c * width), (deep, width))
-    pieces = {0: tile(me)}
-    for s in order:
-        pieces[s] = shift(tile((me + s) % n), s)
-    regrouped = jnp.zeros((n * deep, width), grad.dtype)
-    blend_half = jnp.zeros((n * deep, width), jnp.bfloat16)
+    outgoing = lax.optimization_barrier([tile((me + s) % n) for s in [0] + order])
+    pieces = {0: outgoing[0]}
+    for s, piece in zip(order, outgoing[1:]):
+        pieces[s] = shift(piece, s)
+    regrouped = fresh((n * deep, width), grad.dtype)
+    blend_half = fresh((n * deep, width), jnp.bfloat16)
     panel_own = None
     for s in [0] + order:
         source = (me - s + n) % n
@@ -60,13 +149,20 @@
             panel_own = partial
         else:
             panel_own = panel_own + shift(partial.astype(jnp.bfloat16), -s).astype(jnp.float32)
-    gram = sum_everywhere(jnp.dot(panel_own.T, panel_own, precision=lax.Precision.HIGHEST))
-    panel = jnp.zeros((n * deep, panel_own.shape[1]), jnp.float32)
-    panel = lax.dynamic_update_slice_in_dim(panel, panel_own, me * deep, 0)
+    panel_own = panel_own.astype(jnp.bfloat16)
+    gram_own = lax.dot_general(panel_own, panel_own, (((0,), (0,)), ((), ())), preferred_element_type=jnp.float32)
+    gram = sum_everywhere(gram_own)
+    gram, panel_own = lax.optimization_barrier((gram, panel_own))
+    arrived = {0: panel_own}
     for s in range(1, n):
-        panel = lax.dynamic_update_slice_in_dim(panel, shift(panel_own, s), (me - s + n) % n * deep, 0)
-    lower_factor = jnp.linalg.cholesky(gram)
-    left_factor = jax.scipy.linalg.solve_triangular(lower_factor, panel.T, lower=True).T
+        arrived[s] = shift(panel_own, s)
+    inverse = inverse_factor(gram)
+    panel = fresh((n * deep, panel_own.shape[1]), jnp.bfloat16)
+    for s in range(n):
+        panel = lax.dynamic_update_slice_in_dim(panel, arrived[s], (me - s + n) % n * deep, 0)
+    left_factor = lax.dot_general(
+        panel.astype(jnp.float32), inverse, (((1,), (1,)), ((), ())), precision=HIGHEST, preferred_element_type=jnp.float32
+    )
     left_half = left_factor.astype(jnp.bfloat16)
     contract_rows = (((0,), (0,)), ((), ()))
     term = lax.dot_general(blend_half, left_half, contract_rows, preferred_element_type=jnp.float32)

time: 948 us -> 703 us (0.74)
  other arithmetic: 181 us -> 49.7 us
  waiting for transfers between devices: 387 us -> 303 us
  Pallas kernels: 0 us -> 38.5 us
  local copies, waits for them, and re-layouts: 46.3 us -> 15.6 us
  matrix products: 103 us -> 75.1 us
    another operation x17 -> x0, other arithmetic: 118 us -> none  [the longest x14 79 us: local(): lower_factor = jnp.linalg.cholesky(gram)]
    ppermute x9, waiting for transfers between devices: 282 us -> 208 us  [shift(): return lax.ppermute(x, 'cols', [(i, (i + s) % n) for i in range(n)])]
    pallas_call x0 -> x4, Pallas kernels: none -> 38.5 us  [the longest x1 38.4 us: inverse_factor(): pl.pallas_call(inverse_factor_kernel, out_shape=jax.ShapeDtypeStruct((siz...]
    another operation x13 -> x0, matrix products: 34 us -> none  [the longest x7 32.2 us: local(): jax.scipy.linalg.solve_triangular(lower_factor, panel.T, lower=True)]
    another operation x19 -> x0, local copies, waits for them, and re-layouts: 22.2 us -> none
    dynamic_slice x0 -> x1, local copies, waits for them, and re-layouts: none -> 11.2 us  [local(): tile = lambda c: lax.dynamic_slice(grad, (0, c * width), (deep, width))]
  transfers between devices with their start and end apart: 18 -> 18, of which waited for: 10 -> 9; matrix products, arithmetic and copies ran while one was open for 9% -> 10% of each run, Pallas kernels for 0% -> 5%
where the time goes in v2:
time: 703 us
  waiting for transfers between devices  303 us (43%)
  starting transfers between devices  195 us (28%)
  matrix products  75.1 us (11%)
  other arithmetic  49.7 us (7%)
  Pallas kernels  38.5 us (5%)
  local copies, waits for them, and re-layouts  15.6 us (2%)
  between operations  14.4 us (2%)
  blocking collectives  11.7 us (2%)
    ppermute x9, waiting for transfers between devices, shift(): return lax.ppermute(x, 'cols', [(i, (i + s) % n) for i in range(n)])  208 us
    ppermute x9, starting transfers between devices, shift(): return lax.ppermute(x, 'cols', [(i, (i + s) % n) for i in range(n)])  187 us
    psum x1, waiting for transfers between devices, local(): projected = lax.psum(term.astype(jnp.bfloat16), 'rows').astype(jnp.float32)  77.9 us
    dynamic_update_slice x4, other arithmetic, local(): lax.dynamic_update_slice_in_dim(blend_half, chunk, source * deep, 0)  41.5 us
    pallas_call x1, Pallas kernels, inverse_factor(): pl.pallas_call(inverse_factor_kernel, out_shape=jax.ShapeDtypeStruct((siz...  38.4 us
    dot_general x1, matrix products, local(): lax.dot_general(left_half, projected_half, contract_cols, preferred_eleme...  30.4 us
    dot_general x4, matrix products, local(): partial = jnp.dot(chunk, right_basis, preferred_element_type=jnp.float32)  27.9 us
    ppermute x8, waiting for transfers between devices, flip(): lax.ppermute(x, axis, [(i, i ^ stride) for i in range(lax.axis_size(axis))])  17.1 us
  transfers between devices with their start and end apart: 18, of which 9 were waited for; matrix products, arithmetic and copies ran while one was open for 10% of the time, Pallas kernels for 5%

profile of v2, /device:TPU:0, one launch (start us, length us, event | category | flops | bytes accessed | tf_op | source)
XLA Modules:
  0.0 702.9 jit_solution(13874166038499901996)
XLA Ops:
  7.3 11.2 %constant_dynamic-slice_fusion.3 = (bf16[896,2048]{1,0:T(8,128)(2,1)}, bf16[896,2048]{1,0:T(8,128)(2,1)}, bf16[896,2048]{1,0:T(8,128)(2,1)}, bf16[896,2048]{1,0:T(8,128)(2,1)}) fusion(bf16[896,8192]{1,0:T(8,128)(2,1)} %param.3, s32[]{:T(128)S(6)} %select_n.134, s32[]{:T(128)S(6)} %select_n.130, s32[]{:T(128)S(6)} %select_n.128, s32[]{:T(128)S(6)} %select_n.132), kind=kLoop, calls=%fused_computation.43 | loop fusion | bytes 29360144 | tf_op jit(solution)/shard_map/dynamic_slice | solution.py:133
  18.5 5.0 collective-permute-start.2
  23.5 1.0 collective-permute-start
  24.5 79.0 %collective-permute-done.2 = bf16[896,2048]{1,0:T(8,128)(2,1)} collective-permute-done((bf16[896,2048]{1,0:T(8,128)(2,1)}, bf16[896,2048]{1,0:T(8,128)(2,1)}, u32[]{:S(2)}, u32[]{:S(2)}) %collective-permute-start.2) | collective-permute-done | bytes 3670048 | tf_op jit(solution)/shard_map/ppermute | solution.py:100
  103.6 7.2 %convolution_convert_fusion.1 = bf16[896,512]{1,0:T(8,128)(2,1)} fusion(bf16[2048,512]{1,0:T(8,128)(2,1)S(1)} %copy-done, bf16[896,2048]{1,0:T(8,128)(2,1)} %collective-permute-done.2, f32[3584,2048]{1,0:T(8,128)} %param.4, s32[]{:T(128)S(6)} %select_n.139), kind=kOutput, calls=%fused_computation.13 | convolution fusion | flops 1885011968 | bytes 14024708 | tf_op jit(solution)/shard_map/dot_general | solution.py:145
  110.8 176.3 %collective-permute-start.5 = (bf16[896,512]{1,0:T(8,128)(2,1)}, bf16[896,512]{1,0:T(8,128)(2,1)S(1)}, u32[]{:S(2)}, u32[]{:S(2)}) collective-permute-start(bf16[896,512]{1,0:T(8,128)(2,1)} %convolution_convert_fusion.1), channel_id=1, source_target_pairs={{0,1},{1,2},{2,3},{3,0},{4,5},{5,6},{6,7},{7,4},{8,9},{9,10},{10,1... | collective-permute-start | bytes 2752520 | tf_op jit(solution)/shard_map/ppermute | solution.py:100
  287.1 7.2 %convolution_convert_fusion.2 = bf16[896,512]{1,0:T(8,128)(2,1)} fusion(bf16[2048,512]{1,0:T(8,128)(2,1)S(1)} %copy-done, bf16[896,2048]{1,0:T(8,128)(2,1)} %collective-permute-done.1, f32[3584,2048]{1,0:T(8,128)} %param.4, s32[]{:T(128)S(6)} %select_n.138), kind=kOutput, calls=%fused_computation.14 | convolution fusion | flops 1885011968 | bytes 14024708 | tf_op jit(solution)/shard_map/dot_general | solution.py:145
  294.3 64.8 %collective-permute-done = bf16[896,2048]{1,0:T(8,128)(2,1)} collective-permute-done((bf16[896,2048]{1,0:T(8,128)(2,1)}, bf16[896,2048]{1,0:T(8,128)(2,1)}, u32[]{:S(2)}, u32[]{:S(2)}) %collective-permute-start) | collective-permute-done | bytes 3670048 | tf_op jit(solution)/shard_map/ppermute | solution.py:100
  359.1 7.2 %convolution_convert_fusion.3 = bf16[896,512]{1,0:T(8,128)(2,1)} fusion(bf16[2048,512]{1,0:T(8,128)(2,1)S(1)} %copy-done, bf16[896,2048]{1,0:T(8,128)(2,1)} %collective-permute-done, f32[3584,2048]{1,0:T(8,128)} %param.4, s32[]{:T(128)S(6)} %select_n.137), kind=kOutput, calls=%fused_computation.15 | convolution fusion | flops 1885011968 | bytes 14024708 | tf_op jit(solution)/shard_map/dot_general | solution.py:145
  366.3 6.3 fusion.4
  372.6 0.9 copy-done.4
  373.5 43.4 %collective-permute-done.3 = bf16[896,512]{1,0:T(8,128)(2,1)} collective-permute-done((bf16[896,512]{1,0:T(8,128)(2,1)}, bf16[896,512]{1,0:T(8,128)(2,1)}, u32[]{:S(2)}, u32[]{:S(2)}) %collective-permute-start.3) | collective-permute-done | bytes 917536 | tf_op jit(solution)/shard_map/ppermute | solution.py:100
  417.0 2.3 add_convert_fusion.4
  419.3 0.7 fusion.5
  420.1 0.1 collective-permute-start.6
  420.2 1.9 collective-permute-done.6
  422.1 0.1 dynamic-slice_add_fusion
  422.2 1.6 collective-permute-start.7
  423.8 6.9 collective-permute-done.7
  430.7 1.6 collective-permute-start.8
  432.3 3.4 collective-permute-done.8
  435.7 0.1 collective-permute-start.9
  435.8 4.9 collective-permute-done.9
  440.8 1.2 collective-permute-start.10
  442.0 10.4 %constant_dynamic-update-slice_fusion.3 = (bf16[3584,2048]{1,0:T(8,128)(2,1)}, bf16[3584,2048]{1,0:T(8,128)(2,1)}) fusion(bf16[3584,2048]{1,0:T(8,128)(2,1)} %shard_map.61, s32[]{:T(128)S(6)} %select_n.136, bf16[896,2048]{1,0:T(8,128)(2,1)} %get-tuple-element.9, f32[3584,2048]{1,0:T(8,128)} %param.4, bf16[3584,2048]{1,0:T(8,128)(2,1)} %shard_map.58), kind=kLoop, calls=%fused_computation.31 | loop fusion | flops 5505024 | bytes 18350084 | tf_op jit(solution)/shard_map/dynamic_update_slice | solution.py:147
  452.4 1.6 collective-permute-start.11
  454.0 10.4 %constant_dynamic-update-slice_fusion.2 = (bf16[3584,2048]{1,0:T(8,128)(2,1)}, bf16[3584,2048]{1,0:T(8,128)(2,1)}) fusion(bf16[3584,2048]{1,0:T(8,128)(2,1)} %get-tuple-element.25, s32[]{:T(128)S(6)} %select_n.137, bf16[896,2048]{1,0:T(8,128)(2,1)} %collective-permute-done, f32[3584,2048]{1,0:T(8,128)} %param.4, bf16[3584,2048]{1,0:T(8,128)(2,1)} %get-tuple-element.26), kind=kLoop, calls=%fused_computation.30 | loop fusion | flops 5505024 | bytes 18350084 | tf_op jit(solution)/shard_map/dynamic_update_slice | solution.py:147
  464.4 1.6 collective-permute-start.12
  466.0 10.4 %constant_dynamic-update-slice_fusion.1 = (bf16[3584,2048]{1,0:T(8,128)(2,1)}, bf16[3584,2048]{1,0:T(8,128)(2,1)}) fusion(bf16[3584,2048]{1,0:T(8,128)(2,1)} %get-tuple-element.23, s32[]{:T(128)S(6)} %select_n.138, bf16[896,2048]{1,0:T(8,128)(2,1)} %collective-permute-done.1, f32[3584,2048]{1,0:T(8,128)} %param.4, bf16[3584,2048]{1,0:T(8,128)(2,1)} %get-tuple-element.24), kind=kLoop, calls=%fused_computation.29 | loop fusion | flops 5505024 | bytes 18350084 | tf_op jit(solution)/shard_map/dynamic_update_slice | solution.py:147
  476.4 0.1 collective-permute-start.13
  476.5 10.4 %constant_dynamic-update-slice_fusion = (bf16[3584,2048]{1,0:T(8,128)(2,1)}, bf16[3584,2048]{1,0:T(8,128)(2,1)}) fusion(bf16[3584,2048]{1,0:T(8,128)(2,1)} %get-tuple-element.21, s32[]{:T(128)S(6)} %select_n.139, bf16[896,2048]{1,0:T(8,128)(2,1)} %collective-permute-done.2, f32[3584,2048]{1,0:T(8,128)} %param.4, bf16[3584,2048]{1,0:T(8,128)(2,1)} %get-tuple-element.22), kind=kLoop, calls=%fused_computation.28 | loop fusion | flops 5505024 | bytes 18350084 | tf_op jit(solution)/shard_map/dynamic_update_slice | solution.py:147
  486.9 0.1 broadcast_select_fusion.1
  487.1 2.2 collective-permute-start.14
  489.4 2.6 collective-permute-start.16
  492.0 38.4 %shard_map.60 = f32[512,512]{1,0:T(8,128)S(1)} custom-call(f32[512,512]{1,0:T(8,128)S(1)} %pad_maximum_fusion.gram_ref), custom_call_target="tpu_custom_call" | custom-call | flops 80000000000 | bytes 2097152 | tf_op jit(solution)/shard_map/pallas_call | solution.py:79
  530.5 0.1 constant_dynamic-update-slice_fusion.7
  530.6 0.1 constant_dynamic-update-slice_fusion.6
  530.6 20.5 %collective-permute-done.15 = bf16[896,512]{1,0:T(8,128)(2,1)S(1)} collective-permute-done((bf16[896,512]{1,0:T(8,128)(2,1)S(1)}, bf16[896,512]{1,0:T(8,128)(2,1)S(1)}, u32[]{:S(2)}, u32[]{:S(2)}) %collective-permute-start.15) | collective-permute-done | bytes 917536 | tf_op jit(solution)/shard_map/ppermute | solution.py:100
  551.1 0.1 constant_dynamic-update-slice_fusion.5
  551.2 0.1 constant_dynamic-update-slice_fusion.4
  551.3 5.9 fusion.6
  557.3 3.0 copy-done.2
  560.3 10.2 %convolution_convert_fusion = bf16[2048,512]{1,0:T(8,128)(2,1)} fusion(bf16[3584,2048]{1,0:T(8,128)(2,1)S(1)} %bitcast.11, f32[3584,512]{1,0:T(8,128)S(1)} %fusion.6), kind=kOutput, calls=%fused_computation.9 | convolution fusion | flops 7519076352 | bytes 24117248 | tf_op jit(solution)/shard_map/dot_general | solution.py:168
  570.6 77.9 %all-reduce.2.cloned.1.call-done = bf16[2048,512]{1,0:T(8,128)(2,1)} async-done(((bf16[2048,512]{1,0:T(8,128)(2,1)}), bf16[2048,512]{1,0:T(8,128)(2,1)}) %all-reduce.2.cloned.1.call-update) | async-done | bytes 2097168 | tf_op jit(solution)/shard_map/psum | solution.py:169
  648.5 2.1 fusion
  650.6 11.7 %psum.15 = f32[512]{0:T(512)S(1)} all-reduce(f32[512]{0:T(512)S(1)} %fusion), channel_id=1, replica_groups=mesh['rows'=8,'cols'=4] {'cols'}, use_global_device_ids=true, to_apply=%region_2.3 | all-reduce | flops 512 | bytes 4096 | tf_op jit(solution)/shard_map/psum | solution.py:170
  662.3 30.4 %multiply_subtract_fusion = f32[3584,2048]{1,0:T(8,128)} fusion(f32[3584,2048]{1,0:T(8,128)} %param.4, bf16[3584,2048]{1,0:T(8,128)(2,1)} %get-tuple-element.20, bf16[2048,512]{1,0:T(8,128)(2,1)} %all-reduce.2.cloned.1.call-done, f32[3584,512]{1,0:T(8,128)} %copy-done.2), kind=kOutput, calls=%fused_computation | convolution fusion | flops 7547387904 | bytes 82837504 | tf_op jit(solution)/shard_map/dot_general | solution.py:174
  692.7 3.3 fusion.1
  (48 shorter events, 0.5 us)
Async XLA Ops:
  7.2 96.4 %copy-start = (bf16[2048,512]{1,0:T(8,128)(2,1)S(1)}, bf16[2048,512]{1,0:T(8,128)(2,1)}, u32[]{:S(2)}) copy-start(bf16[2048,512]{1,0:T(8,128)(2,1)} %param.5) | copy-start | bytes 6291460
  7.2 641.3 %all-reduce.2.cloned.1.call-start = ((), (), s32[]{:S(2)}) async-start(), calls=%async_computation | async-start | bytes 4194304 | tf_op jit(solution)/shard_map/psum | solution.py:169
  18.5 85.1 %collective-permute-start.2 = (bf16[896,2048]{1,0:T(8,128)(2,1)}, bf16[896,2048]{1,0:T(8,128)(2,1)}, u32[]{:S(2)}, u32[]{:S(2)}) collective-permute-start(bf16[896,2048]{1,0:T(8,128)(2,1)} %get-tuple-element.12), channel_id=1, source_target_pairs={{0,3},{1,0},{2,1},{3,2},{4,7},{5,4},{6,5},{7,6},{8,11},{9,8},{10,9... | collective-permute-start | bytes 11010056 | tf_op jit(solution)/shard_map/ppermute | solution.py:100
  23.5 263.6 %collective-permute-start.1 = (bf16[896,2048]{1,0:T(8,128)(2,1)}, bf16[896,2048]{1,0:T(8,128)(2,1)}, u32[]{:S(2)}, u32[]{:S(2)}) collective-permute-start(bf16[896,2048]{1,0:T(8,128)(2,1)} %get-tuple-element.11), channel_id=1, source_target_pairs={{0,1},{1,2},{2,3},{3,0},{4,5},{5,6},{6,7},{7,4},{8,9},{9,10},{10,1... | collective-permute-start | bytes 11010056 | tf_op jit(solution)/shard_map/ppermute | solution.py:100
  23.5 335.6 %collective-permute-start = (bf16[896,2048]{1,0:T(8,128)(2,1)}, bf16[896,2048]{1,0:T(8,128)(2,1)}, u32[]{:S(2)}, u32[]{:S(2)}) collective-permute-start(bf16[896,2048]{1,0:T(8,128)(2,1)} %get-tuple-element.10), channel_id=1, source_target_pairs={{0,2},{1,3},{2,0},{3,1},{4,6},{5,7},{6,4},{7,5},{8,10},{9,11},{10,... | collective-permute-start | bytes 11010056 | tf_op jit(solution)/shard_map/ppermute | solution.py:100
  110.8 261.8 %collective-permute-start.5 = (bf16[896,512]{1,0:T(8,128)(2,1)}, bf16[896,512]{1,0:T(8,128)(2,1)S(1)}, u32[]{:S(2)}, u32[]{:S(2)}) collective-permute-start(bf16[896,512]{1,0:T(8,128)(2,1)} %convolution_convert_fusion.1), channel_id=1, source_target_pairs={{0,1},{1,2},{2,3},{3,0},{4,5},{5,6},{6,7},{7,4},{8,9},{9,10},{10,1... | collective-permute-start | bytes 2752520 | tf_op jit(solution)/shard_map/ppermute | solution.py:100
  294.3 78.3 %collective-permute-start.4 = (bf16[896,512]{1,0:T(8,128)(2,1)}, bf16[896,512]{1,0:T(8,128)(2,1)}, u32[]{:S(2)}, u32[]{:S(2)}) collective-permute-start(bf16[896,512]{1,0:T(8,128)(2,1)} %convolution_convert_fusion.2), channel_id=1, source_target_pairs={{0,3},{1,0},{2,1},{3,2},{4,7},{5,4},{6,5},{7,6},{8,11},{9,8},{10,9... | collective-permute-start | bytes 2752520 | tf_op jit(solution)/shard_map/ppermute | solution.py:100
  366.3 50.6 %collective-permute-start.3 = (bf16[896,512]{1,0:T(8,128)(2,1)}, bf16[896,512]{1,0:T(8,128)(2,1)}, u32[]{:S(2)}, u32[]{:S(2)}) collective-permute-start(bf16[896,512]{1,0:T(8,128)(2,1)} %convolution_convert_fusion.3), channel_id=1, source_target_pairs={{0,2},{1,3},{2,0},{3,1},{4,6},{5,7},{6,4},{7,5},{8,10},{9,11},{10,... | collective-permute-start | bytes 2752520 | tf_op jit(solution)/shard_map/ppermute | solution.py:100
  372.6 0.9 copy-start.4
  420.1 2.0 collective-permute-start.6
  422.2 8.4 %collective-permute-start.7 = (f32[128,512]{1,0:T(8,128)S(1)}, f32[128,512]{1,0:T(8,128)S(1)}, u32[]{:S(2)}, u32[]{:S(2)}) collective-permute-start(f32[128,512]{1,0:T(8,128)S(1)} %constant_dynamic-slice_fusion.1), channel_id=1, source_target_pairs={{0,8},{4,12},{8,0},{12,4},{16,24},{20,28},{24,16},{28,20},{1,9},{5... | collective-permute-start | bytes 786440 | tf_op jit(solution)/shard_map/ppermute | solution.py:104
  430.7 5.0 collective-permute-start.8
  435.7 5.0 collective-permute-start.9
  440.8 11.6 %collective-permute-start.10 = (f32[64,512]{1,0:T(8,128)S(1)}, f32[64,512]{1,0:T(8,128)S(1)}, u32[]{:S(2)}, u32[]{:S(2)}) collective-permute-start(f32[64,512]{1,0:T(8,128)S(1)} %add.188), channel_id=1, source_target_pairs={{0,2},{1,3},{2,0},{3,1},{4,6},{5,7},{6,4},{7,5},{8,10},{9,11},{10,... | collective-permute-start | bytes 393224 | tf_op jit(solution)/shard_map/ppermute | solution.py:104
  452.4 11.9 %collective-permute-start.11 = (f32[64,512]{1,0:T(8,128)S(1)}, f32[64,512]{1,0:T(8,128)S(1)}, u32[]{:S(2)}, u32[]{:S(2)}) collective-permute-start(f32[64,512]{1,0:T(8,128)S(1)} %add.189), channel_id=1, source_target_pairs={{0,16},{4,20},{8,24},{12,28},{16,0},{20,4},{24,8},{28,12},{1,17},{... | collective-permute-start | bytes 393224 | tf_op jit(solution)/shard_map/ppermute | solution.py:104
  464.4 11.9 %collective-permute-start.12 = (f32[128,512]{1,0:T(8,128)S(1)}, f32[128,512]{1,0:T(8,128)S(1)}, u32[]{:S(2)}, u32[]{:S(2)}) collective-permute-start(f32[128,512]{1,0:T(8,128)S(1)} %pad_maximum_fusion.2), channel_id=1, source_target_pairs={{0,8},{4,12},{8,0},{12,4},{16,24},{20,28},{24,16},{28,20},{1,9},{5... | collective-permute-start | bytes 786440 | tf_op jit(solution)/shard_map/ppermute | solution.py:104
  476.4 10.5 %collective-permute-start.13 = (f32[256,512]{1,0:T(8,128)S(1)}, f32[256,512]{1,0:T(8,128)S(1)}, u32[]{:S(2)}, u32[]{:S(2)}) collective-permute-start(f32[256,512]{1,0:T(8,128)S(1)} %pad_maximum_fusion.1), channel_id=1, source_target_pairs={{0,4},{4,0},{8,12},{12,8},{16,20},{20,16},{24,28},{28,24},{1,5},{5... | collective-permute-start | bytes 1572872 | tf_op jit(solution)/shard_map/ppermute | solution.py:104
  486.9 73.4 %slice-start = ((s8[14680064]{0:T(1024)(128)(4,1)}), s8[4194304]{0:T(1024)(128)(4,1)S(1)}, s32[]{:S(2)}) async-start(s8[14680064]{0:T(1024)(128)(4,1)} %bitcast.10), calls=%async_computation.1 | async-start | bytes 8388608
  487.1 43.4 %copy-start.3 = (bf16[3584,512]{1,0:T(8,128)(2,1)S(1)}, bf16[3584,512]{1,0:T(8,128)(2,1)}, u32[]{:S(2)}) copy-start(bf16[3584,512]{1,0:T(8,128)(2,1)} %shard_map.59) | copy-start | bytes 11010052
  487.1 73.2 %slice-start.1 = ((s8[14680064]{0:T(1024)(128)(4,1)}), s8[4194304]{0:T(1024)(128)(4,1)S(1)}, s32[]{:S(2)}) async-start(s8[14680064]{0:T(1024)(128)(4,1)} %bitcast.10), calls=%async_computation.2 | async-start | bytes 8388608
  487.1 73.2 %slice-start.2 = ((s8[14680064]{0:T(1024)(128)(4,1)}), s8[4194304]{0:T(1024)(128)(4,1)S(1)}, s32[]{:S(2)}) async-start(s8[14680064]{0:T(1024)(128)(4,1)} %bitcast.10), calls=%async_computation.3 | async-start | bytes 8388608
  487.1 73.2 %slice-start.3 = ((s8[14680064]{0:T(1024)(128)(4,1)}), s8[2097152]{0:T(1024)(128)(4,1)S(1)}, s32[]{:S(2)}) async-start(s8[14680064]{0:T(1024)(128)(4,1)} %bitcast.10), calls=%async_computation.4 | async-start | bytes 4194304
  487.1 43.4 %collective-permute-start.14 = (bf16[896,512]{1,0:T(8,128)(2,1)S(1)}, bf16[896,512]{1,0:T(8,128)(2,1)S(1)}, u32[]{:S(2)}, u32[]{:S(2)}) collective-permute-start(bf16[896,512]{1,0:T(8,128)(2,1)S(1)} %add_convert_fusion.4), channel_id=1, source_target_pairs={{0,1},{1,2},{2,3},{3,0},{4,5},{5,6},{6,7},{7,4},{8,9},{9,10},{10,1... | collective-permute-start | bytes 2752520 | tf_op jit(solution)/shard_map/ppermute | solution.py:100
  489.3 61.8 %collective-permute-start.15 = (bf16[896,512]{1,0:T(8,128)(2,1)S(1)}, bf16[896,512]{1,0:T(8,128)(2,1)S(1)}, u32[]{:S(2)}, u32[]{:S(2)}) collective-permute-start(bf16[896,512]{1,0:T(8,128)(2,1)S(1)} %add_convert_fusion.4), channel_id=1, source_target_pairs={{0,2},{1,3},{2,0},{3,1},{4,6},{5,7},{6,4},{7,5},{8,10},{9,11},{10,... | collective-permute-start | bytes 2752520 | tf_op jit(solution)/shard_map/ppermute | solution.py:100
  489.4 61.9 %collective-permute-start.16 = (bf16[896,512]{1,0:T(8,128)(2,1)S(1)}, bf16[896,512]{1,0:T(8,128)(2,1)S(1)}, u32[]{:S(2)}, u32[]{:S(2)}) collective-permute-start(bf16[896,512]{1,0:T(8,128)(2,1)S(1)} %add_convert_fusion.4), channel_id=1, source_target_pairs={{0,3},{1,0},{2,1},{3,2},{4,7},{5,4},{6,5},{7,6},{8,11},{9,8},{10,9... | collective-permute-start | bytes 2752520 | tf_op jit(solution)/shard_map/ppermute | solution.py:100
  557.3 3.1 copy-start.2
  662.3 33.7 %copy-start.1 = (bf16[2048,512]{1,0:T(8,128)(2,1)S(1)}, bf16[2048,512]{1,0:T(8,128)(2,1)}, u32[]{:S(2)}) copy-start(bf16[2048,512]{1,0:T(8,128)(2,1)} %param.5) | copy-start | bytes 6291460
Sparse Core Ops, SparseCore 0:
  570.7 77.7 all-reduce.1

commit v3 on v2

--- a/solution.py
+++ b/solution.py
@@ -104,24 +104,46 @@
     return lax.ppermute(x, axis, [(i, i ^ stride) for i in range(lax.axis_size(axis))])
 
 
-def sum_everywhere(x):
-    levels = lax.axis_size("rows").bit_length() - 1
+def halve(x, levels, sent):
     index = lax.axis_index("rows")
-    for level in range(levels):
+    for level in levels:
         bit = (index >> level) & 1
         half = x.shape[0] // 2
         keep = lax.dynamic_slice_in_dim(x, bit * half, half)
         send = lax.dynamic_slice_in_dim(x, (1 - bit) * half, half)
-        x = keep + flip(send, "rows", 1 << level)
-    for level in range(lax.axis_size("cols").bit_length() - 1):
-        x = x + flip(x, "cols", 1 << level)
-    for level in reversed(range(levels)):
+        x = keep + flip(send.astype(sent), "rows", 1 << level).astype(x.dtype)
+    return x
+
+
+def double(x, levels):
+    index = lax.axis_index("rows")
+    for level in reversed(levels):
         bit = (index >> level) & 1
         other = flip(x, "rows", 1 << level)
         low = jnp.where(bit == 0, x, other)
         high = jnp.where(bit == 0, other, x)
         x = jnp.concatenate([low, high], axis=0)
     return x
+
+
+def butterfly(x, axis):
+    for level in range(lax.axis_size(axis).bit_length() - 1):
+        x = x + flip(x, axis, 1 << level)
+    return x
+
+
+def sum_everywhere(x):
+    levels = list(range(lax.axis_size("rows").bit_length() - 1))
+    return double(butterfly(halve(x, levels, x.dtype), "cols"), levels)
+
+
+def sum_rows(x):
+    levels = list(range(lax.axis_size("rows").bit_length() - 1))
+    half = x.shape[0] // 2
+    orders = (levels, levels[:1] + levels[:0:-1])
+    parts = [halve(x[i * half:(i + 1) * half], order, jnp.bfloat16) for i, order in enumerate(orders)]
+    parts = [double(part.astype(jnp.bfloat16), order) for part, order in zip(parts, orders)]
+    return jnp.concatenate(parts, axis=0)
 
 
 def local(grad, momentum, right_basis):
@@ -150,6 +172,7 @@
         else:
             panel_own = panel_own + shift(partial.astype(jnp.bfloat16), -s).astype(jnp.float32)
     panel_own = panel_own.astype(jnp.bfloat16)
+    panel_own, regrouped, blend_half = lax.optimization_barrier((panel_own, regrouped, blend_half))
     gram_own = lax.dot_general(panel_own, panel_own, (((0,), (0,)), ((), ())), preferred_element_type=jnp.float32)
     gram = sum_everywhere(gram_own)
     gram, panel_own = lax.optimization_barrier((gram, panel_own))
@@ -166,8 +189,8 @@
     left_half = left_factor.astype(jnp.bfloat16)
     contract_rows = (((0,), (0,)), ((), ()))
     term = lax.dot_general(blend_half, left_half, contract_rows, preferred_element_type=jnp.float32)
-    projected = lax.psum(term.astype(jnp.bfloat16), "rows").astype(jnp.float32)
-    column_sums = lax.psum(jnp.sum(projected * projected, axis=0), "cols")
+    projected = sum_rows(term).astype(jnp.float32)
+    column_sums = butterfly(jnp.sum(projected * projected, axis=0), "cols")
     projected_half = projected.astype(jnp.bfloat16)
     right_new = (projected / jnp.sqrt(column_sums + epsilon)).astype(jnp.bfloat16)
     contract_cols = (((1,), (1,)), ((), ()))

time: 703 us -> 647 us (0.920)
  starting transfers between devices: 195 us -> 161 us
  between operations: 14.4 us -> 1.75 us
  blocking collectives: 11.7 us -> 0 us
    psum x1 -> x0, waiting for transfers between devices: 77.9 us -> none  [local(): projected = lax.psum(term.astype(jnp.bfloat16), 'rows').astype(jnp.float32)]
    ppermute x9, starting transfers between devices: 187 us -> 123 us  [shift(): return lax.ppermute(x, 'cols', [(i, (i + s) % n) for i in range(n)])]
    ppermute x8 -> x22, waiting for transfers between devices: 17.1 us -> 56.2 us  [flip(): lax.ppermute(x, axis, [(i, i ^ stride) for i in range(lax.axis_size(axis))])]
    ppermute x9, waiting for transfers between devices: 208 us -> 247 us  [shift(): return lax.ppermute(x, 'cols', [(i, (i + s) % n) for i in range(n)])]
    ppermute x8 -> x22, starting transfers between devices: 7.72 us -> 37.8 us  [flip(): lax.ppermute(x, axis, [(i, i ^ stride) for i in range(lax.axis_size(axis))])]
    psum x1 -> x0, blocking collectives: 11.7 us -> none  [local(): column_sums = lax.psum(jnp.sum(projected * projected, axis=0), 'cols')]
  transfers between devices with their start and end apart: 18 -> 31, of which waited for: 9 -> 22; matrix products, arithmetic and copies ran while one was open for 10% -> 15% of each run, Pallas kernels for 5% -> 6%
where the time goes in v3:
time: 647 us; the launch traced here: 640 us
  waiting for transfers between devices  303 us (47%)
  starting transfers between devices  161 us (25%)
  matrix products  70.5 us (11%)
  other arithmetic  49.4 us (8%)
  Pallas kernels  38.4 us (6%)
  local copies, waits for them, and re-layouts  16.7 us (3%)
    ppermute x9, waiting for transfers between devices, shift(): return lax.ppermute(x, 'cols', [(i, (i + s) % n) for i in range(n)])  247 us
    ppermute x9, starting transfers between devices, shift(): return lax.ppermute(x, 'cols', [(i, (i + s) % n) for i in range(n)])  123 us
    ppermute x22, waiting for transfers between devices, flip(): lax.ppermute(x, axis, [(i, i ^ stride) for i in range(lax.axis_size(axis))])  56.2 us
    dynamic_update_slice x4, other arithmetic, local(): lax.dynamic_update_slice_in_dim(blend_half, chunk, source * deep, 0)  39.3 us
    pallas_call x1, Pallas kernels, inverse_factor(): pl.pallas_call(inverse_factor_kernel, out_shape=jax.ShapeDtypeStruct((siz...  38.4 us
    ppermute x22, starting transfers between devices, flip(): lax.ppermute(x, axis, [(i, i ^ stride) for i in range(lax.axis_size(axis))])  37.8 us
    dot_general x1, matrix products, local(): lax.dot_general(left_half, projected_half, contract_cols, preferred_eleme...  28.2 us
    dot_general x4, matrix products, local(): partial = jnp.dot(chunk, right_basis, preferred_element_type=jnp.float32)  25.2 us
  transfers between devices with their start and end apart: 31, of which 22 were waited for; matrix products, arithmetic and copies ran while one was open for 15% of the time, Pallas kernels for 6%

profile of v3, /device:TPU:0, one launch (start us, length us, event | category | flops | bytes accessed | tf_op | source)
XLA Modules:
  0.0 640.4 jit_solution(17939571132176561360)
XLA Ops:
  0.7 11.2 %constant_dynamic-slice_fusion.3 = (bf16[896,2048]{1,0:T(8,128)(2,1)}, bf16[896,2048]{1,0:T(8,128)(2,1)}, bf16[896,2048]{1,0:T(8,128)(2,1)}, bf16[896,2048]{1,0:T(8,128)(2,1)}) fusion(bf16[896,8192]{1,0:T(8,128)(2,1)} %param.3, s32[]{:T(128)S(6)} %select_n.226, s32[]{:T(128)S(6)} %select_n.222, s32[]{:T(128)S(6)} %select_n.220, s32[]{:T(128)S(6)} %select_n.224), kind=kLoop, calls=%fused_computation.72 | loop fusion | bytes 29360144 | tf_op jit(solution)/shard_map/dynamic_slice | solution.py:155
  11.9 4.0 collective-permute-start
  16.0 1.6 collective-permute-start.2
  17.6 2.2 collective-permute-start.4
  19.8 6.4 %fusion.5 = f32[896,512]{1,0:T(8,128)S(1)} fusion(bf16[2048,512]{1,0:T(8,128)(2,1)S(1)} %copy-done, bf16[896,2048]{1,0:T(8,128)(2,1)} %get-tuple-element.12, f32[3584,2048]{1,0:T(8,128)} %param.4, s32[]{:T(128)S(6)} %select_n.218), kind=kOutput, calls=%fused_computation.77 | convolution fusion | flops 1884553216 | bytes 14942212 | tf_op jit(solution)/shard_map/dot_general | solution.py:167
  26.2 8.2 %constant_dynamic-update-slice_fusion.7 = (bf16[3584,2048]{1,0:T(8,128)(2,1)}, bf16[3584,2048]{1,0:T(8,128)(2,1)}) fusion(bf16[3584,2048]{1,0:T(8,128)(2,1)} %shard_map.59, s32[]{:T(128)S(6)} %select_n.218, bf16[896,2048]{1,0:T(8,128)(2,1)S(1)} %copy-done.4, f32[3584,2048]{1,0:T(8,128)} %param.4, bf16[3584,2048]{1,0:T(8,128)(2,1)} %shard_map.58), kind=kLoop, calls=%fused_computation.67 | loop fusion | flops 5505024 | bytes 18350084 | tf_op jit(solution)/shard_map/dynamic_update_slice | solution.py:169
  34.4 220.2 %collective-permute-done = bf16[896,2048]{1,0:T(8,128)(2,1)} collective-permute-done((bf16[896,2048]{1,0:T(8,128)(2,1)}, bf16[896,2048]{1,0:T(8,128)(2,1)}, u32[]{:S(2)}, u32[]{:S(2)}) %collective-permute-start) | collective-permute-done | bytes 3670048 | tf_op jit(solution)/shard_map/ppermute | solution.py:100
  254.6 6.3 convolution_convert_fusion.2
  261.0 6.3 convolution_convert_fusion.1
  267.3 6.3 convolution_convert_fusion
  273.6 111.0 %collective-permute-start.5 = (bf16[896,512]{1,0:T(8,128)(2,1)S(1)}, bf16[896,512]{1,0:T(8,128)(2,1)S(1)}, u32[]{:S(2)}, u32[]{:S(2)}) collective-permute-start(bf16[896,512]{1,0:T(8,128)(2,1)S(1)} %convolution_convert_fusion), channel_id=1, source_target_pairs={{0,1},{1,2},{2,3},{3,0},{4,5},{5,6},{6,7},{7,4},{8,9},{9,10},{10,1... | collective-permute-start | bytes 2752520 | tf_op jit(solution)/shard_map/ppermute | solution.py:100
  384.6 10.4 %constant_dynamic-update-slice_fusion.6 = (bf16[3584,2048]{1,0:T(8,128)(2,1)}, bf16[3584,2048]{1,0:T(8,128)(2,1)}) fusion(bf16[3584,2048]{1,0:T(8,128)(2,1)} %get-tuple-element.33, s32[]{:T(128)S(6)} %select_n.227, bf16[896,2048]{1,0:T(8,128)(2,1)} %collective-permute-done, f32[3584,2048]{1,0:T(8,128)} %param.4, bf16[3584,2048]{1,0:T(8,128)(2,1)} %get-tuple-element.34), kind=kLoop, calls=%fused_computation.66 | loop fusion | flops 5505024 | bytes 18350084 | tf_op jit(solution)/shard_map/dynamic_update_slice | solution.py:169
  394.9 10.4 %constant_dynamic-update-slice_fusion.5 = (bf16[3584,2048]{1,0:T(8,128)(2,1)}, bf16[3584,2048]{1,0:T(8,128)(2,1)}) fusion(bf16[3584,2048]{1,0:T(8,128)(2,1)} %get-tuple-element.31, s32[]{:T(128)S(6)} %select_n.228, bf16[896,2048]{1,0:T(8,128)(2,1)} %collective-permute-done.2, f32[3584,2048]{1,0:T(8,128)} %param.4, bf16[3584,2048]{1,0:T(8,128)(2,1)} %get-tuple-element.32), kind=kLoop, calls=%fused_computation.65 | loop fusion | flops 5505024 | bytes 18350084 | tf_op jit(solution)/shard_map/dynamic_update_slice | solution.py:169
  405.3 10.4 %constant_dynamic-update-slice_fusion.4 = (bf16[3584,2048]{1,0:T(8,128)(2,1)}, bf16[3584,2048]{1,0:T(8,128)(2,1)}) fusion(bf16[3584,2048]{1,0:T(8,128)(2,1)} %get-tuple-element.29, s32[]{:T(128)S(6)} %select_n.229, bf16[896,2048]{1,0:T(8,128)(2,1)} %collective-permute-done.4, f32[3584,2048]{1,0:T(8,128)} %param.4, bf16[3584,2048]{1,0:T(8,128)(2,1)} %get-tuple-element.30), kind=kLoop, calls=%fused_computation.64 | loop fusion | flops 5505024 | bytes 18350084 | tf_op jit(solution)/shard_map/dynamic_update_slice | solution.py:169
  415.7 5.6 collective-permute-done.5
  422.6 1.9 collective-permute-done.6
  424.6 1.5 collective-permute-start.7
  426.2 6.9 %collective-permute-done.7 = f32[128,512]{1,0:T(8,128)S(1)} collective-permute-done((f32[128,512]{1,0:T(8,128)S(1)}, f32[128,512]{1,0:T(8,128)S(1)}, u32[]{:S(2)}, u32[]{:S(2)}) %collective-permute-start.7) | collective-permute-done | bytes 262176 | tf_op jit(solution)/shard_map/ppermute | solution.py:104
  433.1 1.6 collective-permute-start.8
  434.7 3.5 collective-permute-done.8
  438.2 5.0 collective-permute-done.9
  443.3 6.7 %collective-permute-done.10 = f32[64,512]{1,0:T(8,128)S(1)} collective-permute-done((f32[64,512]{1,0:T(8,128)S(1)}, f32[64,512]{1,0:T(8,128)S(1)}, u32[]{:S(2)}, u32[]{:S(2)}) %collective-permute-start.10) | collective-permute-done | bytes 131104 | tf_op jit(solution)/shard_map/ppermute | solution.py:104
  450.0 1.6 collective-permute-start.11
  451.6 3.5 collective-permute-done.11
  456.6 4.9 collective-permute-done.12
  461.7 1.9 collective-permute-done.13
  464.0 3.9 collective-permute-start.16
  467.9 38.4 %shard_map.61 = f32[512,512]{1,0:T(8,128)S(1)} custom-call(f32[512,512]{1,0:T(8,128)S(1)} %pad_maximum_fusion.1.gram_ref), custom_call_target="tpu_custom_call" | custom-call | flops 80000000000 | bytes 2097152 | tf_op jit(solution)/shard_map/pallas_call | solution.py:79
  506.6 20.9 %collective-permute-done.15 = bf16[896,512]{1,0:T(8,128)(2,1)S(1)} collective-permute-done((bf16[896,512]{1,0:T(8,128)(2,1)S(1)}, bf16[896,512]{1,0:T(8,128)(2,1)S(1)}, u32[]{:S(2)}, u32[]{:S(2)}) %collective-permute-start.15) | collective-permute-done | bytes 917536 | tf_op jit(solution)/shard_map/ppermute | solution.py:100
  527.6 5.9 fusion.8
  533.6 10.4 %fusion.3 = f32[2048,512]{1,0:T(8,128)} fusion(bf16[3584,2048]{1,0:T(8,128)(2,1)S(1)} %bitcast.10, f32[3584,512]{1,0:T(8,128)S(1)} %fusion.8), kind=kOutput, calls=%fused_computation.11 | convolution fusion | flops 7518027776 | bytes 26214400 | tf_op jit(solution)/shard_map/dot_general | solution.py:191
  544.0 2.7 fusion.6
  551.8 1.5 collective-permute-start.18
  554.6 1.6 collective-permute-start.24
  556.2 4.0 collective-permute-done.18
  560.3 1.6 collective-permute-start.19
  563.6 1.9 collective-permute-done.19
  565.6 1.6 collective-permute-start.20
  568.7 1.9 collective-permute-done.20
  572.0 2.7 collective-permute-done.26
  574.7 1.6 collective-permute-start.27
  576.4 1.7 collective-permute-done.21
  578.3 2.9 collective-permute-done.27
  581.6 1.7 collective-permute-done.28
  584.9 19.4 %collective-permute-start.29 = (f32[512]{0:T(512)S(1)}, f32[512]{0:T(512)S(1)}, u32[]{:S(2)}, u32[]{:S(2)}) collective-permute-start(f32[512]{0:T(512)S(1)} %fusion), channel_id=1, source_target_pairs={{0,1},{1,0},{2,3},{3,2},{4,5},{5,4},{6,7},{7,6},{8,9},{9,8},{10,11... | collective-permute-start | bytes 6152 | tf_op jit(solution)/shard_map/ppermute | solution.py:104
  604.3 1.6 collective-permute-done.29
  606.8 28.2 %multiply_subtract_fusion = f32[3584,2048]{1,0:T(8,128)} fusion(f32[3584,2048]{1,0:T(8,128)} %param.4, bf16[3584,2048]{1,0:T(8,128)(2,1)} %get-tuple-element.16, f32[3584,512]{1,0:T(8,128)} %copy-done.2, bf16[512,512]{1,0:T(8,128)(2,1)} %copy-done.6, bf16[512,512]{1,0:T(8,128)(2,1)} %copy-done.5, bf16[512,512]{1,0:T(8,128)(2,1)S(1)} %get-tuple-element.36, ...), kind=kOutput, calls=%fused_computation | convolution fusion | flops 7555776512 | bytes 82837504 | tf_op jit(solution)/shard_map/dot_general | solution.py:197
  635.0 4.9 fusion.1
  (102 shorter events, 18.4 us)
Async XLA Ops:
  0.6 19.2 %copy-start = (bf16[2048,512]{1,0:T(8,128)(2,1)S(1)}, bf16[2048,512]{1,0:T(8,128)(2,1)}, u32[]{:S(2)}) copy-start(bf16[2048,512]{1,0:T(8,128)(2,1)} %param.5) | copy-start | bytes 6291460
  11.9 242.7 %collective-permute-start = (bf16[896,2048]{1,0:T(8,128)(2,1)}, bf16[896,2048]{1,0:T(8,128)(2,1)}, u32[]{:S(2)}, u32[]{:S(2)}) collective-permute-start(bf16[896,2048]{1,0:T(8,128)(2,1)} %get-tuple-element.13), channel_id=1, source_target_pairs={{0,2},{1,3},{2,0},{3,1},{4,6},{5,7},{6,4},{7,5},{8,10},{9,11},{10,... | collective-permute-start | bytes 11010056 | tf_op jit(solution)/shard_map/ppermute | solution.py:100
  16.0 245.0 %collective-permute-start.2 = (bf16[896,2048]{1,0:T(8,128)(2,1)}, bf16[896,2048]{1,0:T(8,128)(2,1)}, u32[]{:S(2)}, u32[]{:S(2)}) collective-permute-start(bf16[896,2048]{1,0:T(8,128)(2,1)} %get-tuple-element.14), channel_id=1, source_target_pairs={{0,1},{1,2},{2,3},{3,0},{4,5},{5,6},{6,7},{7,4},{8,9},{9,10},{10,1... | collective-permute-start | bytes 11010056 | tf_op jit(solution)/shard_map/ppermute | solution.py:100
  17.6 249.8 %collective-permute-start.4 = (bf16[896,2048]{1,0:T(8,128)(2,1)}, bf16[896,2048]{1,0:T(8,128)(2,1)}, u32[]{:S(2)}, u32[]{:S(2)}) collective-permute-start(bf16[896,2048]{1,0:T(8,128)(2,1)} %get-tuple-element.15), channel_id=1, source_target_pairs={{0,3},{1,0},{2,1},{3,2},{4,7},{5,4},{6,5},{7,6},{8,11},{9,8},{10,9... | collective-permute-start | bytes 11010056 | tf_op jit(solution)/shard_map/ppermute | solution.py:100
  19.8 6.4 %copy-start.4 = (bf16[896,2048]{1,0:T(8,128)(2,1)S(1)}, bf16[896,2048]{1,0:T(8,128)(2,1)}, u32[]{:S(2)}) copy-start(bf16[896,2048]{1,0:T(8,128)(2,1)} %get-tuple-element.12) | copy-start | bytes 11010052
  260.9 154.8 %collective-permute-start.1 = (bf16[896,512]{1,0:T(8,128)(2,1)S(1)}, bf16[896,512]{1,0:T(8,128)(2,1)S(1)}, u32[]{:S(2)}, u32[]{:S(2)}) collective-permute-start(bf16[896,512]{1,0:T(8,128)(2,1)S(1)} %convolution_convert_fusion.2), channel_id=1, source_target_pairs={{0,2},{1,3},{2,0},{3,1},{4,6},{5,7},{6,4},{7,5},{8,10},{9,11},{10,... | collective-permute-start | bytes 2752520 | tf_op jit(solution)/shard_map/ppermute | solution.py:100
  267.2 148.4 %collective-permute-start.3 = (bf16[896,512]{1,0:T(8,128)(2,1)S(1)}, bf16[896,512]{1,0:T(8,128)(2,1)S(1)}, u32[]{:S(2)}, u32[]{:S(2)}) collective-permute-start(bf16[896,512]{1,0:T(8,128)(2,1)S(1)} %convolution_convert_fusion.1), channel_id=1, source_target_pairs={{0,3},{1,0},{2,1},{3,2},{4,7},{5,4},{6,5},{7,6},{8,11},{9,8},{10,9... | collective-permute-start | bytes 2752520 | tf_op jit(solution)/shard_map/ppermute | solution.py:100
  273.6 147.6 %collective-permute-start.5 = (bf16[896,512]{1,0:T(8,128)(2,1)S(1)}, bf16[896,512]{1,0:T(8,128)(2,1)S(1)}, u32[]{:S(2)}, u32[]{:S(2)}) collective-permute-start(bf16[896,512]{1,0:T(8,128)(2,1)S(1)} %convolution_convert_fusion), channel_id=1, source_target_pairs={{0,1},{1,2},{2,3},{3,0},{4,5},{5,6},{6,7},{7,4},{8,9},{9,10},{10,1... | collective-permute-start | bytes 2752520 | tf_op jit(solution)/shard_map/ppermute | solution.py:100
  422.5 2.0 collective-permute-start.6
  424.6 8.4 %collective-permute-start.7 = (f32[128,512]{1,0:T(8,128)S(1)}, f32[128,512]{1,0:T(8,128)S(1)}, u32[]{:S(2)}, u32[]{:S(2)}) collective-permute-start(f32[128,512]{1,0:T(8,128)S(1)} %constant_dynamic-slice_fusion.1), channel_id=1, source_target_pairs={{0,8},{4,12},{8,0},{12,4},{16,24},{20,28},{24,16},{28,20},{1,9},{5... | collective-permute-start | bytes 786440 | tf_op jit(solution)/shard_map/ppermute | solution.py:104
  433.1 5.0 collective-permute-start.8
  438.2 5.0 collective-permute-start.9
  443.2 6.8 %collective-permute-start.10 = (f32[64,512]{1,0:T(8,128)S(1)}, f32[64,512]{1,0:T(8,128)S(1)}, u32[]{:S(2)}, u32[]{:S(2)}) collective-permute-start(f32[64,512]{1,0:T(8,128)S(1)} %add.236), channel_id=1, source_target_pairs={{0,2},{1,3},{2,0},{3,1},{4,6},{5,7},{6,4},{7,5},{8,10},{9,11},{10,... | collective-permute-start | bytes 393224 | tf_op jit(solution)/shard_map/ppermute | solution.py:104
  450.0 5.0 collective-permute-start.11
  455.1 6.4 %collective-permute-start.12 = (f32[128,512]{1,0:T(8,128)S(1)}, f32[128,512]{1,0:T(8,128)S(1)}, u32[]{:S(2)}, u32[]{:S(2)}) collective-permute-start(f32[128,512]{1,0:T(8,128)S(1)} %pad_maximum_fusion.5), channel_id=1, source_target_pairs={{0,8},{4,12},{8,0},{12,4},{16,24},{20,28},{24,16},{28,20},{1,9},{5... | collective-permute-start | bytes 786440 | tf_op jit(solution)/shard_map/ppermute | solution.py:104
  461.6 2.0 collective-permute-start.13
  463.6 69.9 %slice-start = ((s8[14680064]{0:T(1024)(128)(4,1)}), s8[4194304]{0:T(1024)(128)(4,1)S(1)}, s32[]{:S(2)}) async-start(s8[14680064]{0:T(1024)(128)(4,1)} %bitcast.9), calls=%async_computation | async-start | bytes 8388608
  463.8 42.6 %copy-start.3 = (bf16[3584,512]{1,0:T(8,128)(2,1)S(1)}, bf16[3584,512]{1,0:T(8,128)(2,1)}, u32[]{:S(2)}) copy-start(bf16[3584,512]{1,0:T(8,128)(2,1)} %shard_map.60) | copy-start | bytes 11010052
  463.8 69.7 %slice-start.1 = ((s8[14680064]{0:T(1024)(128)(4,1)}), s8[4194304]{0:T(1024)(128)(4,1)S(1)}, s32[]{:S(2)}) async-start(s8[14680064]{0:T(1024)(128)(4,1)} %bitcast.9), calls=%async_computation.1 | async-start | bytes 8388608
  463.8 69.7 %slice-start.2 = ((s8[14680064]{0:T(1024)(128)(4,1)}), s8[4194304]{0:T(1024)(128)(4,1)S(1)}, s32[]{:S(2)}) async-start(s8[14680064]{0:T(1024)(128)(4,1)} %bitcast.9), calls=%async_computation.2 | async-start | bytes 8388608
  463.8 69.7 %slice-start.3 = ((s8[14680064]{0:T(1024)(128)(4,1)}), s8[2097152]{0:T(1024)(128)(4,1)S(1)}, s32[]{:S(2)}) async-start(s8[14680064]{0:T(1024)(128)(4,1)} %bitcast.9), calls=%async_computation.3 | async-start | bytes 4194304
  463.9 42.6 %collective-permute-start.14 = (bf16[896,512]{1,0:T(8,128)(2,1)S(1)}, bf16[896,512]{1,0:T(8,128)(2,1)S(1)}, u32[]{:S(2)}, u32[]{:S(2)}) collective-permute-start(bf16[896,512]{1,0:T(8,128)(2,1)S(1)} %add_convert_fusion.4), channel_id=1, source_target_pairs={{0,1},{1,2},{2,3},{3,0},{4,5},{5,6},{6,7},{7,4},{8,9},{9,10},{10,1... | collective-permute-start | bytes 2752520 | tf_op jit(solution)/shard_map/ppermute | solution.py:100
  463.9 63.5 %collective-permute-start.15 = (bf16[896,512]{1,0:T(8,128)(2,1)S(1)}, bf16[896,512]{1,0:T(8,128)(2,1)S(1)}, u32[]{:S(2)}, u32[]{:S(2)}) collective-permute-start(bf16[896,512]{1,0:T(8,128)(2,1)S(1)} %add_convert_fusion.4), channel_id=1, source_target_pairs={{0,2},{1,3},{2,0},{3,1},{4,6},{5,7},{6,4},{7,5},{8,10},{9,11},{10,... | collective-permute-start | bytes 2752520 | tf_op jit(solution)/shard_map/ppermute | solution.py:100
  464.0 63.5 %collective-permute-start.16 = (bf16[896,512]{1,0:T(8,128)(2,1)S(1)}, bf16[896,512]{1,0:T(8,128)(2,1)S(1)}, u32[]{:S(2)}, u32[]{:S(2)}) collective-permute-start(bf16[896,512]{1,0:T(8,128)(2,1)S(1)} %add_convert_fusion.4), channel_id=1, source_target_pairs={{0,3},{1,0},{2,1},{3,2},{4,7},{5,4},{6,5},{7,6},{8,11},{9,8},{10,9... | collective-permute-start | bytes 2752520 | tf_op jit(solution)/shard_map/ppermute | solution.py:100
  533.6 10.4 %copy-start.2 = (f32[3584,512]{1,0:T(8,128)}, f32[3584,512]{1,0:T(8,128)S(1)}, u32[]{:S(2)}) copy-start(f32[3584,512]{1,0:T(8,128)S(1)} %fusion.8) | copy-start | bytes 22020100
  546.7 1.3 copy-start.7
  548.1 2.1 collective-permute-start.17
  548.2 5.1 collective-permute-start.23
  551.8 8.4 %collective-permute-start.18 = (bf16[256,512]{1,0:T(8,128)(2,1)S(1)}, bf16[256,512]{1,0:T(8,128)(2,1)S(1)}, u32[]{:S(2)}, u32[]{:S(2)}) collective-permute-start(bf16[256,512]{1,0:T(8,128)(2,1)S(1)} %dynamic-slice_convert_fusion.3), channel_id=1, source_target_pairs={{0,8},{4,12},{8,0},{12,4},{16,24},{20,28},{24,16},{28,20},{1,9},{5... | collective-permute-start | bytes 786440 | tf_op jit(solution)/shard_map/ppermute | solution.py:104
  554.6 8.5 %collective-permute-start.24 = (bf16[256,512]{1,0:T(8,128)(2,1)S(1)}, bf16[256,512]{1,0:T(8,128)(2,1)S(1)}, u32[]{:S(2)}, u32[]{:S(2)}) collective-permute-start(bf16[256,512]{1,0:T(8,128)(2,1)S(1)} %dynamic-slice_convert_fusion.2), channel_id=1, source_target_pairs={{0,16},{4,20},{8,24},{12,28},{16,0},{20,4},{24,8},{28,12},{1,17},{... | collective-permute-start | bytes 786440 | tf_op jit(solution)/shard_map/ppermute | solution.py:104
  560.3 5.2 collective-permute-start.19
  563.2 5.0 collective-permute-start.25
  565.6 5.0 collective-permute-start.20
  568.3 6.4 %collective-permute-start.26 = (bf16[128,512]{1,0:T(8,128)(2,1)S(1)}, bf16[128,512]{1,0:T(8,128)(2,1)S(1)}, u32[]{:S(2)}, u32[]{:S(2)}) collective-permute-start(bf16[128,512]{1,0:T(8,128)(2,1)S(1)} %add_convert_fusion.5), channel_id=1, source_target_pairs={{0,8},{4,12},{8,0},{12,4},{16,24},{20,28},{24,16},{28,20},{1,9},{5... | collective-permute-start | bytes 393224 | tf_op jit(solution)/shard_map/ppermute | solution.py:104
  570.7 7.4 %collective-permute-start.21 = (bf16[256,512]{1,0:T(8,128)(2,1)S(1)}, bf16[256,512]{1,0:T(8,128)(2,1)S(1)}, u32[]{:S(2)}, u32[]{:S(2)}) collective-permute-start(bf16[256,512]{1,0:T(8,128)(2,1)S(1)} %pad_maximum_fusion.6), channel_id=1, source_target_pairs={{0,8},{4,12},{8,0},{12,4},{16,24},{20,28},{24,16},{28,20},{1,9},{5... | collective-permute-start | bytes 786440 | tf_op jit(solution)/shard_map/ppermute | solution.py:104
  574.7 6.4 %collective-permute-start.27 = (bf16[256,512]{1,0:T(8,128)(2,1)S(1)}, bf16[256,512]{1,0:T(8,128)(2,1)S(1)}, u32[]{:S(2)}, u32[]{:S(2)}) collective-permute-start(bf16[256,512]{1,0:T(8,128)(2,1)S(1)} %pad_maximum_fusion.7), channel_id=1, source_target_pairs={{0,16},{4,20},{8,24},{12,28},{16,0},{20,4},{24,8},{28,12},{1,17},{... | collective-permute-start | bytes 786440 | tf_op jit(solution)/shard_map/ppermute | solution.py:104
  578.2 3.2 collective-permute-start.22
  581.3 2.0 collective-permute-start.28
  583.5 0.8 copy-start.5
  583.5 1.4 copy-start.6
  584.9 21.0 %collective-permute-start.29 = (f32[512]{0:T(512)S(1)}, f32[512]{0:T(512)S(1)}, u32[]{:S(2)}, u32[]{:S(2)}) collective-permute-start(f32[512]{0:T(512)S(1)} %fusion), channel_id=1, source_target_pairs={{0,1},{1,0},{2,3},{3,2},{4,5},{5,4},{6,7},{7,6},{8,9},{9,8},{10,11... | collective-permute-start | bytes 6152 | tf_op jit(solution)/shard_map/ppermute | solution.py:104
  605.8 29.2 %collective-permute-start.30 = (f32[512]{0:T(512)S(1)}, f32[512]{0:T(512)S(1)}, u32[]{:S(2)}, u32[]{:S(2)}) collective-permute-start(f32[512]{0:T(512)S(1)} %add.252), channel_id=1, source_target_pairs={{0,2},{1,3},{2,0},{3,1},{4,6},{5,7},{6,4},{7,5},{8,10},{9,11},{10,... | collective-permute-start | bytes 6152 | tf_op jit(solution)/shard_map/ppermute | solution.py:104
  606.8 33.1 %copy-start.1 = (bf16[2048,512]{1,0:T(8,128)(2,1)S(1)}, bf16[2048,512]{1,0:T(8,128)(2,1)}, u32[]{:S(2)}) copy-start(bf16[2048,512]{1,0:T(8,128)(2,1)} %param.5) | copy-start | bytes 6291460
